TPU v7x, 32 devices: a whole 2x2x4 slice. The times are simulated.
32 devices in a mesh: dp: 4 (over z), fsdp: 8 (over y, x, core).
Axes of the slice: x: 2, y: 2, z: 4, core: 2. Of those that a mesh axis runs over, the one named last changes fastest.
Arguments:
- tokens: bfloat16 [32768, 768], P(('dp', 'fsdp')), may hold values from -6 to 6
- cotangent: bfloat16 [32768, 768], P(('dp', 'fsdp')), may hold values from -6 to 6
- bucket: int32 [64], P(('dp', 'fsdp')), may hold values from 0 to 2, as said below
- lengths: int32 [64, 4], P(('dp', 'fsdp')), may hold values from 0 to 512, as said below
- w_query: bfloat16 [768, 768], P('fsdp'), may hold values from -0.3125 to 0.3125
- b_query: bfloat16 [768], P('fsdp'), may hold values from -2 to 2
- w_key: bfloat16 [768, 768], P('fsdp'), may hold values from -0.3125 to 0.3125
- w_value: bfloat16 [768, 768], P('fsdp'), may hold values from -0.21875 to 0.21875
- b_value: bfloat16 [768], P('fsdp'), may hold values from -2 to 2
- w_out: bfloat16 [768, 768], P('fsdp'), may hold values from -1.25 to 1.25
- b_out: bfloat16 [768], P('fsdp'), may hold values from -2 to 2
- gain_one: bfloat16 [768], P('fsdp'), may hold values from 0.5 to 1.5
- shift_one: bfloat16 [768], P('fsdp'), may hold values from -2 to 2
- w_up: bfloat16 [768, 3072], P('fsdp'), may hold values from -0.21875 to 0.21875
- b_up: bfloat16 [3072], P('fsdp'), may hold values from -2 to 2
- w_down: bfloat16 [3072, 768], P('fsdp'), may hold values from -0.109375 to 0.109375
- b_down: bfloat16 [768], P('fsdp'), may hold values from -2 to 2
- gain_two: bfloat16 [768], P('fsdp'), may hold values from 0.5 to 1.5
- shift_two: bfloat16 [768], P('fsdp'), may hold values from -2 to 2
Outputs:
- output: bfloat16 [32768, 768], P(('dp', 'fsdp'))
- grad_tokens: float32 [32768, 768], P(('dp', 'fsdp'))
- grad_w_query: float32 [768, 768], P('fsdp')
- grad_b_query: float32 [768], P('fsdp')
- grad_w_key: float32 [768, 768], P('fsdp')
- grad_w_value: float32 [768, 768], P('fsdp')
- grad_b_value: float32 [768], P('fsdp')
- grad_w_out: float32 [768, 768], P('fsdp')
- grad_b_out: float32 [768], P('fsdp')
- grad_gain_one: float32 [768], P('fsdp')
- grad_shift_one: float32 [768], P('fsdp')
- grad_w_up: float32 [768, 3072], P('fsdp')
- grad_b_up: float32 [3072], P('fsdp')
- grad_w_down: float32 [3072, 768], P('fsdp')
- grad_b_down: float32 [768], P('fsdp')
- grad_gain_two: float32 [768], P('fsdp')
- grad_shift_two: float32 [768], P('fsdp')
Inputs may be any that keep to these rules, and one draw needn't show every extreme that they name: bucket b gives micro-batch segments of 512 >> (2 - b) tokens; bucket[0] is 2. For a micro-batch of bucket b, entries 0 to (1 << (2 - b)) - 1 are its sequences' lengths, each from a quarter of its segment to the whole segment; the other entries are 0; lengths[0, 0] is 512.
All inputs are finite; a program needn't handle non-finite values.
Results may differ from a plain program's by a relative error of at most 0.02.
Values may be sent and summed in bfloat16 or wider, within the bound.
No kernel may reach another device: no remote copies, remote signals or barrier semaphores. Data moves between devices by JAX's collectives and lax.ppermute only.
A program may use at most 192 MiB of HBM per device.

v0:
```python
import jax
import jax.numpy as jnp
from jax import lax
from jax.sharding import PartitionSpec as P

D = 768
H = 12
HD = 64


MASKED = -1000000000.0
EPSILON = 1e-05


def for_sending(x):
    return jax.tree.map(lambda a: a.astype(jnp.bfloat16) if a.dtype == jnp.float32 else a, x)


def key_mask(bucket_id, seq_lens, slot_count):
    seg_len = jnp.right_shift(jnp.int32(slot_count), 2 - bucket_id)
    where_at = jnp.arange(slot_count, dtype=jnp.int32)
    seg_id = where_at // seg_len
    inside = where_at - seg_id * seg_len
    choose = seg_id[:, None] == jnp.arange(4, dtype=jnp.int32)[None, :]
    limits = jnp.sum(jnp.where(choose, seq_lens[None, :], 0), axis=1)
    live_rows = inside < limits
    allowed = (seg_id[:, None] == seg_id[None, :]) & live_rows[None, :]
    return (allowed, live_rows)


def layer_norm(row_data, gain_vec, shift_vec):
    row_mean = jnp.mean(row_data, axis=-1, keepdims=True)
    centered = row_data - row_mean
    variance = jnp.mean(centered * centered, axis=-1, keepdims=True)
    return centered * lax.rsqrt(variance + EPSILON) * gain_vec + shift_vec


def gelu_exact(inputs_pre):
    return jax.nn.gelu(inputs_pre, approximate=False)


def project(inputs_low, matrix, offset):
    return jnp.dot(inputs_low, matrix, preferred_element_type=jnp.float32) + offset.astype(
        jnp.float32
    )


def head_scores(query_low, key_low, allowed):
    scores = (
        jnp.einsum("qhd,khd->hqk", query_low, key_low, preferred_element_type=jnp.float32) * 0.125
    )
    return jnp.where(allowed[None], scores, MASKED)


def forward(weights, tok_rows, allowed):
    (
        w_query,
        b_query,
        w_key,
        w_value,
        b_value,
        w_out,
        b_out,
        gain_one,
        shift_one,
        w_up,
        b_up,
        w_down,
        b_down,
        gain_two,
        shift_two,
    ) = weights
    slot_count = tok_rows.shape[0]
    query_low = project(tok_rows, w_query, b_query).astype(jnp.bfloat16).reshape(slot_count, H, HD)
    key_low = (
        jnp.dot(tok_rows, w_key, preferred_element_type=jnp.float32)
        .astype(jnp.bfloat16)
        .reshape(slot_count, H, HD)
    )
    value_low = project(tok_rows, w_value, b_value).astype(jnp.bfloat16).reshape(slot_count, H, HD)
    scores = head_scores(query_low, key_low, allowed)
    row_max = jnp.max(scores, axis=-1, keepdims=True)
    exp_scores = jnp.exp(scores - row_max)
    row_total = jnp.sum(exp_scores, axis=-1, keepdims=True)
    attn_probs = exp_scores / row_total
    log_total = row_max + jnp.log(row_total)
    context = (
        jnp.einsum(
            "hqk,khd->qhd",
            attn_probs.astype(jnp.bfloat16),
            value_low,
            preferred_element_type=jnp.float32,
        )
        .reshape(slot_count, D)
        .astype(jnp.bfloat16)
    )
    resid_one = tok_rows.astype(jnp.float32) + project(context, w_out, b_out)
    hidden, norm_one = jax.vjp(
        layer_norm, resid_one, gain_one.astype(jnp.float32), shift_one.astype(jnp.float32)
    )
    hidden_low = hidden.astype(jnp.bfloat16)
    upward = project(hidden_low, w_up, b_up)
    active, gelu_back = jax.vjp(gelu_exact, upward)
    active_low = active.astype(jnp.bfloat16)
    resid_two = hidden + project(active_low, w_down, b_down)
    output, norm_two = jax.vjp(
        layer_norm, resid_two, gain_two.astype(jnp.float32), shift_two.astype(jnp.float32)
    )
    kept = (
        query_low,
        key_low,
        value_low,
        log_total,
        context,
        norm_one,
        hidden_low,
        gelu_back,
        active_low,
        norm_two,
    )
    return (output.astype(jnp.bfloat16), kept)


def backward(weights, tok_rows, allowed, live_rows, cot_rows, kept):
    (
        w_query,
        b_query,
        w_key,
        w_value,
        b_value,
        w_out,
        b_out,
        gain_one,
        shift_one,
        w_up,
        b_up,
        w_down,
        b_down,
        gain_two,
        shift_two,
    ) = weights
    (
        query_low,
        key_low,
        value_low,
        log_total,
        context,
        norm_one,
        hidden_low,
        gelu_back,
        active_low,
        norm_two,
    ) = kept
    slot_count = tok_rows.shape[0]
    grad_rows = cot_rows.astype(jnp.float32) * live_rows[:, None].astype(jnp.float32)
    d_resid_two, g_gain_two, g_shift_two = norm_two(grad_rows)
    d_down = d_resid_two.astype(jnp.bfloat16)
    g_b_down = jnp.sum(d_down.astype(jnp.float32), axis=0)
    g_w_down = jnp.einsum("tf,td->fd", active_low, d_down, preferred_element_type=jnp.float32)
    d_active = jnp.einsum("td,fd->tf", d_down, w_down, preferred_element_type=jnp.float32)
    (d_upward,) = gelu_back(d_active)
    d_up_low = d_upward.astype(jnp.bfloat16)
    g_b_up = jnp.sum(d_up_low.astype(jnp.float32), axis=0)
    g_w_up = jnp.einsum("td,tf->df", hidden_low, d_up_low, preferred_element_type=jnp.float32)
    d_hidden = d_resid_two + jnp.einsum(
        "tf,df->td", d_up_low, w_up, preferred_element_type=jnp.float32
    )
    d_resid_one, g_gain_one, g_shift_one = norm_one(d_hidden)
    d_attended = d_resid_one.astype(jnp.bfloat16)
    g_b_out = jnp.sum(d_attended.astype(jnp.float32), axis=0)
    g_w_out = jnp.einsum("td,te->de", context, d_attended, preferred_element_type=jnp.float32)
    d_context = (
        jnp.einsum("te,de->td", d_attended, w_out, preferred_element_type=jnp.float32)
        .astype(jnp.bfloat16)
        .reshape(slot_count, H, HD)
    )
    attn_probs = jnp.exp(head_scores(query_low, key_low, allowed) - log_total)
    d_values = (
        jnp.einsum(
            "hqk,qhd->khd",
            attn_probs.astype(jnp.bfloat16),
            d_context,
            preferred_element_type=jnp.float32,
        )
        .reshape(slot_count, D)
        .astype(jnp.bfloat16)
    )
    d_probs = jnp.einsum("qhd,khd->hqk", d_context, value_low, preferred_element_type=jnp.float32)
    d_scores = (
        attn_probs * (d_probs - jnp.sum(attn_probs * d_probs, axis=-1, keepdims=True))
    ).astype(jnp.bfloat16)
    d_query = (
        (jnp.einsum("hqk,khd->qhd", d_scores, key_low, preferred_element_type=jnp.float32) * 0.125)
        .reshape(slot_count, D)
        .astype(jnp.bfloat16)
    )
    d_keys = (
        (
            jnp.einsum("hqk,qhd->khd", d_scores, query_low, preferred_element_type=jnp.float32)
            * 0.125
        )
        .reshape(slot_count, D)
        .astype(jnp.bfloat16)
    )
    g_b_query = jnp.sum(d_query.astype(jnp.float32), axis=0)
    g_b_value = jnp.sum(d_values.astype(jnp.float32), axis=0)
    g_w_query = jnp.einsum("td,te->de", tok_rows, d_query, preferred_element_type=jnp.float32)
    g_w_key = jnp.einsum("td,te->de", tok_rows, d_keys, preferred_element_type=jnp.float32)
    g_w_value = jnp.einsum("td,te->de", tok_rows, d_values, preferred_element_type=jnp.float32)
    d_tokens = (
        d_resid_one
        + jnp.einsum("te,de->td", d_query, w_query, preferred_element_type=jnp.float32)
        + jnp.einsum("te,de->td", d_keys, w_key, preferred_element_type=jnp.float32)
        + jnp.einsum("te,de->td", d_values, w_value, preferred_element_type=jnp.float32)
    )
    gradients = (
        g_w_query,
        g_b_query,
        g_w_key,
        g_w_value,
        g_b_value,
        g_w_out,
        g_b_out,
        g_gain_one,
        g_shift_one,
        g_w_up,
        g_b_up,
        g_w_down,
        g_b_down,
        g_gain_two,
        g_shift_two,
    )
    return (d_tokens, gradients)


def on_device(
    tokens,
    cotangent,
    bucket,
    lengths,
    w_query,
    b_query,
    w_key,
    w_value,
    b_value,
    w_out,
    b_out,
    gain_one,
    shift_one,
    w_up,
    b_up,
    w_down,
    b_down,
    gain_two,
    shift_two,
):
    shards = (
        w_query,
        b_query,
        w_key,
        w_value,
        b_value,
        w_out,
        b_out,
        gain_one,
        shift_one,
        w_up,
        b_up,
        w_down,
        b_down,
        gain_two,
        shift_two,
    )
    micro_count = bucket.shape[0]
    slot_count = tokens.shape[0] // micro_count
    summed_full = None
    owned_sums = None
    outputs = []
    token_grads = []
    for micro_idx in range(micro_count):
        tok_rows = lax.slice_in_dim(
            tokens, micro_idx * slot_count, (micro_idx + 1) * slot_count, axis=0
        )
        cot_rows = lax.slice_in_dim(
            cotangent, micro_idx * slot_count, (micro_idx + 1) * slot_count, axis=0
        )
        allowed, live_rows = key_mask(bucket[micro_idx], lengths[micro_idx], slot_count)
        fwd_weights = (
            lax.all_gather(shards[0], "fsdp", axis=0, tiled=True),
            lax.all_gather(shards[1], "fsdp", axis=0, tiled=True),
            lax.all_gather(shards[2], "fsdp", axis=0, tiled=True),
            lax.all_gather(shards[3], "fsdp", axis=0, tiled=True),
            lax.all_gather(shards[4], "fsdp", axis=0, tiled=True),
            lax.all_gather(shards[5], "fsdp", axis=0, tiled=True),
            lax.all_gather(shards[6], "fsdp", axis=0, tiled=True),
            lax.all_gather(shards[7], "fsdp", axis=0, tiled=True),
            lax.all_gather(shards[8], "fsdp", axis=0, tiled=True),
            lax.all_gather(shards[9], "fsdp", axis=0, tiled=True),
            lax.all_gather(shards[10], "fsdp", axis=0, tiled=True),
            lax.all_gather(shards[11], "fsdp", axis=0, tiled=True),
            lax.all_gather(shards[12], "fsdp", axis=0, tiled=True),
            lax.all_gather(shards[13], "fsdp", axis=0, tiled=True),
            lax.all_gather(shards[14], "fsdp", axis=0, tiled=True),
        )
        output, kept = forward(fwd_weights, tok_rows, allowed)
        outputs.append(output)
        back_weights = (
            lax.all_gather(shards[0], "fsdp", axis=0, tiled=True),
            lax.all_gather(shards[1], "fsdp", axis=0, tiled=True),
            lax.all_gather(shards[2], "fsdp", axis=0, tiled=True),
            lax.all_gather(shards[3], "fsdp", axis=0, tiled=True),
            lax.all_gather(shards[4], "fsdp", axis=0, tiled=True),
            lax.all_gather(shards[5], "fsdp", axis=0, tiled=True),
            lax.all_gather(shards[6], "fsdp", axis=0, tiled=True),
            lax.all_gather(shards[7], "fsdp", axis=0, tiled=True),
            lax.all_gather(shards[8], "fsdp", axis=0, tiled=True),
            lax.all_gather(shards[9], "fsdp", axis=0, tiled=True),
            lax.all_gather(shards[10], "fsdp", axis=0, tiled=True),
            lax.all_gather(shards[11], "fsdp", axis=0, tiled=True),
            lax.all_gather(shards[12], "fsdp", axis=0, tiled=True),
            lax.all_gather(shards[13], "fsdp", axis=0, tiled=True),
            lax.all_gather(shards[14], "fsdp", axis=0, tiled=True),
        )
        d_tokens, gradients = backward(back_weights, tok_rows, allowed, live_rows, cot_rows, kept)
        token_grads.append(d_tokens)
        summed_full = (
            gradients if summed_full is None else jax.tree.map(jnp.add, summed_full, gradients)
        )
    owned_sums = jax.tree.map(
        lambda part: part.astype(jnp.float32),
        lax.psum_scatter(for_sending(summed_full), "fsdp", scatter_dimension=0, tiled=True),
    )
    finals = jax.tree.map(
        lambda part: part.astype(jnp.float32), lax.psum(for_sending(owned_sums), "dp")
    )
    return (jnp.concatenate(outputs, axis=0), jnp.concatenate(token_grads, axis=0)) + tuple(finals)


def solution(mesh):
    placed = (
        P(("dp", "fsdp"), None),
        P(("dp", "fsdp"), None),
        P(("dp", "fsdp")),
        P(("dp", "fsdp"), None),
        P("fsdp", None),
        P("fsdp"),
        P("fsdp", None),
        P("fsdp", None),
        P("fsdp"),
        P("fsdp", None),
        P("fsdp"),
        P("fsdp"),
        P("fsdp"),
        P("fsdp", None),
        P("fsdp"),
        P("fsdp", None),
        P("fsdp"),
        P("fsdp"),
        P("fsdp"),
    )
    return jax.shard_map(
        on_device,
        mesh=mesh,
        in_specs=placed,
        out_specs=(
            P(("dp", "fsdp"), None),
            P(("dp", "fsdp"), None),
            P("fsdp", None),
            P("fsdp"),
            P("fsdp", None),
            P("fsdp", None),
            P("fsdp"),
            P("fsdp", None),
            P("fsdp"),
            P("fsdp"),
            P("fsdp"),
            P("fsdp", None),
            P("fsdp"),
            P("fsdp", None),
            P("fsdp"),
            P("fsdp"),
            P("fsdp"),
        ),
        check_vma=False,
    )
```

profile of v0, /device:TPU:0, one launch (start us, length us, event | category | flops | bytes accessed | tf_op | source)
XLA Modules:
  0.0 682.6 jit_solution(5053814164061390214)
XLA Ops:
  23.4 25.7 %all-reduce.18 = (bf16[768]{0:T(1024)(128)(2,1)S(1)}, bf16[768]{0:T(1024)(128)(2,1)S(1)}, bf16[768]{0:T(1024)(128)(2,1)S(1)}, bf16[768]{0:T(1024)(128)(2,1)S(1)}...) all-reduce(bf16[768]{0:T(1024)(128)(2,1)S(1)} %dynamic-update-slice, ...), channel_id=1, replica_groups=mesh['dp'=4,'fsdp'=8] {'fsdp'}, use_global_device_ids=true, to_apply=%add | all-reduce | flops 5376 | bytes 21504
  51.2 8.6 %all-gather = bf16[8,1,384]{2,1,0:T(2,128)(2,1)S(1)} all-gather(bf16[1,1,384]{2,1,0:T(2,128)(2,1)S(1)} %reshape.453), channel_id=1, replica_groups=mesh['dp'=4,'fsdp'=8] {'fsdp'}, dimensions={0}, use_global_device_ids=true | all-gather | bytes 6912 | tf_op jit(solution)/shard_map/all_gather | solution.py:299
  61.1 2.6 add_convert_fusion.9
  68.0 3.0 add_convert_fusion.10
  75.0 2.3 copy.101
  77.4 11.1 %all-gather.12.cloned.1.call-done = bf16[768,768]{1,0:T(8,128)(2,1)} async-done(((bf16[96,768]{1,0:T(8,128)(2,1)}), bf16[768,768]{1,0:T(8,128)(2,1)}) %all-gather.12.cloned.1.call-update) | async-done | bytes 1179664 | tf_op jit(solution)/shard_map/all_gather | solution.py:291
  90.8 3.2 convolution_convert_fusion.3
  95.4 3.5 fusion.24
  99.0 3.8 fusion
  103.7 5.6 fusion.40
  109.4 4.8 all-gather.14.cloned.1.call-done
  114.1 2.5 fusion.91
  119.9 2.6 fusion.1
  125.0 3.6 fusion.39
  130.7 24.0 %all-gather.16.cloned.1.call-done = bf16[768,3072]{1,0:T(8,128)(2,1)} async-done(((bf16[96,3072]{1,0:T(8,128)(2,1)}), bf16[768,3072]{1,0:T(8,128)(2,1)}) %all-gather.16.cloned.1.call-update) | async-done | bytes 4718608 | tf_op jit(solution)/shard_map/all_gather | solution.py:298
  154.7 5.3 fusion.75
  160.0 2.6 copy-done.111
  162.6 35.0 %multiply_convert_fusion.3 = (bf16[512,3072]{1,0:T(8,128)(2,1)}, f32[512,3072]{1,0:T(8,128)}, bf16[512,3072]{1,0:T(8,128)(2,1)}, f32[512,3072]{1,0:T(8,128)}, f32[512,3072]{1,0:T(8,128)}) fusion(f32[3072]{0:T(1024)S(1)} %bitcast.160, f32[512,3072]{1,0:T(8,128)S(1)} %fusion.75, bf16[768,3072]{1,0:T(8,128)(2,1)S(1)} %copy-done.102, ...), kind=kOutput, calls=%fused_computation.43 | convolution fusion | flops 2625503232 | bytes 37771264 | tf_op jit(solution)/shard_map/dot_general | solution.py:43
  197.6 6.2 fusion.93
  204.2 2.8 fusion.94
  214.7 4.5 fusion.95
  219.3 18.7 %convert_reduce_fusion = (f32[3072]{0:T(1024)}, bf16[512,3072]{1,0:T(8,128)(2,1)}, f32[3072]{0:T(1024)}, bf16[512,3072]{1,0:T(8,128)(2,1)}) fusion(f32[512,3072]{1,0:T(8,128)} %get-tuple-element.164, f32[512,3072]{1,0:T(8,128)} %copy-done.111, f32[3072]{0:T(1024)S(1)} %bitcast.161, f32[512,3072]{1,0:T(8,128)} %fusion.95, ...), kind=kOutput, calls=%fused_computation.24 | convolution fusion | flops 2469390336 | bytes 43290624 | tf_op jit(solution)/shard_map/td,fd->tf/dot_general | solution.py:160
  237.9 6.5 add_add_fusion.11
  244.5 6.4 multiply_reduce_fusion.4
  260.1 9.6 %convert_reduce_fusion.7 = (f32[12,64]{1,0:T(8,128)}, bf16[12,64,512]{2,1,0:T(8,128)(2,1)}) fusion(bf16[512,12,64]{0,2,1:T(8,128)(2,1)} %bitcast.144, f32[12,512]{1,0:T(8,128)S(1)} %copy-done.61, f32[12,512,512]{1,2,0:T(8,128)} %copy-done, pred[512,512]{0,1:T(8,128)(4,1)S(1)} %copy-done.21), kind=kOutput, calls=%fused_computation.81 | convolution fusion | flops 416414976 | bytes 14445568 | tf_op jit(solution)/shard_map/hqk,qhd->khd/dot_general | solution.py:179
  269.7 9.6 %multiply_reduce_fusion.1 = (f32[12,512]{1,0:T(8,128)S(1)}, f32[12,512,512]{1,2,0:T(8,128)}) fusion(f32[12,512]{1,0:T(8,128)S(1)} %copy-done.61, f32[12,512,512]{1,2,0:T(8,128)} %copy-done, pred[512,512]{0,1:T(8,128)(4,1)S(1)} %copy-done.21, bf16[512,12,64]{0,2,1:T(8,128)(2,1)S(1)} %bitcast.145, bf16[512,12,64]{0,2,1:T(8,128)(2,1)S(1)} %bitcast.143), kind=kOutput, calls=%fused_computation.4 | convolution fusion | flops 418375680 | bytes 27049984 | tf_op jit(solution)/shard_map/qhd,khd->hqk/dot_general | solution.py:188
  285.6 8.7 %convert_reduce_fusion.6 = (f32[12,64]{1,0:T(8,128)}, bf16[12,64,512]{2,1,0:T(8,128)(2,1)S(1)}) fusion(bf16[512,12,64]{0,2,1:T(8,128)(2,1)} %bitcast.146, f32[12,512]{1,0:T(8,128)S(1)} %copy-done.62, f32[12,512,512]{1,2,0:T(8,128)} %copy-done.1, pred[512,512]{0,1:T(8,128)(4,1)S(1)} %copy-done.19), kind=kOutput, calls=%fused_computation.80 | convolution fusion | flops 416414976 | bytes 14445568 | tf_op jit(solution)/shard_map/hqk,qhd->khd/dot_general | solution.py:179
  294.3 9.9 %multiply_reduce_fusion = (f32[12,512]{1,0:T(8,128)S(1)}, f32[12,512,512]{1,2,0:T(8,128)}) fusion(f32[12,512]{1,0:T(8,128)S(1)} %copy-done.62, f32[12,512,512]{1,2,0:T(8,128)} %copy-done.1, pred[512,512]{0,1:T(8,128)(4,1)S(1)} %copy-done.19, bf16[512,12,64]{0,2,1:T(8,128)(2,1)S(1)} %bitcast.147, bf16[512,12,64]{0,2,1:T(8,128)(2,1)S(1)} %bitcast.141), kind=kOutput, calls=%fused_computation.1 | convolution fusion | flops 418375680 | bytes 27049984 | tf_op jit(solution)/shard_map/qhd,khd->hqk/dot_general | solution.py:188
  306.8 2.4 copy.132
  309.3 10.8 %multiply_convert_fusion.1 = bf16[12,512,512]{1,2,0:T(8,128)(2,1)S(1)} fusion(f32[12,512,512]{1,2,0:T(8,128)} %get-tuple-element.193, f32[12,512]{1,0:T(8,128)S(1)} %get-tuple-element.192, f32[12,512]{1,0:T(8,128)S(1)} %copy-done.61, f32[12,512,512]{1,2,0:T(8,128)} %copy-done, pred[512,512]{0,1:T(8,128)(4,1)} %compare_and_fusion.1), kind=kLoop, calls=%fused_computation.3 | loop fusion | flops 18874368 | bytes 31768576 | tf_op jit(solution)/shard_map/convert_element_type | solution.py:191
  325.7 7.1 %multiply_convert_fusion = bf16[12,512,512]{1,2,0:T(8,128)(2,1)S(1)} fusion(f32[12,512,512]{1,2,0:T(8,128)} %get-tuple-element.197, f32[12,512]{1,0:T(8,128)S(1)} %get-tuple-element.196, f32[12,512]{1,0:T(8,128)S(1)} %copy-done.62, f32[12,512,512]{1,2,0:T(8,128)S(1)} %bitcast.127, pred[512,512]{0,1:T(8,128)(4,1)S(1)} %copy-done.19), kind=kLoop, calls=%fused_computation | loop fusion | flops 18874368 | bytes 31768576 | tf_op jit(solution)/shard_map/convert_element_type | solution.py:191
  338.1 2.4 copy.130
  341.0 4.3 convert_reduce_fusion.9
  347.0 3.9 convert_reduce_fusion.8
  353.6 2.4 copy.128
  356.1 2.3 fusion.100
  360.3 5.0 fusion.101
  365.3 4.6 add_convert_fusion
  370.6 5.4 fusion.77
  376.0 4.9 add_convert_fusion.1
  383.1 23.9 %all-reduce.17 = (bf16[768]{0:T(1024)(128)(2,1)S(1)}, bf16[768]{0:T(1024)(128)(2,1)S(1)}, bf16[768]{0:T(1024)(128)(2,1)S(1)}, bf16[768]{0:T(1024)(128)(2,1)S(1)}...) all-reduce(bf16[768]{0:T(1024)(128)(2,1)S(1)} %dynamic-update-slice, ...), channel_id=1, replica_groups=mesh['dp'=4,'fsdp'=8] {'fsdp'}, use_global_device_ids=true, to_apply=%add.7 | all-reduce | flops 9984 | bytes 39936
  407.0 3.6 fusion.96
  417.9 8.7 %reduce-scatter.19.cloned.1.call-done = bf16[96,768]{1,0:T(8,128)(2,1)} async-done(((bf16[768,768]{1,0:T(8,128)(2,1)}), bf16[96,768]{1,0:T(8,128)(2,1)}) %reduce-scatter.19.cloned.1.call-update) | async-done | bytes 147472
  428.3 38.6 %reduce-scatter.13.cloned.1.call-done = bf16[96,768]{1,0:T(8,128)(2,1)} async-done(((bf16[768,768]{1,0:T(8,128)(2,1)}), bf16[96,768]{1,0:T(8,128)(2,1)}) %reduce-scatter.13.cloned.1.call-update) | async-done | bytes 147472 | tf_op jit(solution)/shard_map/reduce_scatter | solution.py:331
  466.9 57.3 %reduce-scatter.17.cloned.1.call-done = bf16[384,768]{1,0:T(8,128)(2,1)} async-done(((bf16[3072,768]{1,0:T(8,128)(2,1)}), bf16[384,768]{1,0:T(8,128)(2,1)}) %reduce-scatter.17.cloned.1.call-update) | async-done | bytes 589840 | tf_op jit(solution)/shard_map/reduce_scatter | solution.py:331
  524.2 57.1 %reduce-scatter.15.cloned.1.call-done = bf16[96,3072]{1,0:T(8,128)(2,1)} async-done(((bf16[768,3072]{1,0:T(8,128)(2,1)}), bf16[96,3072]{1,0:T(8,128)(2,1)}) %reduce-scatter.15.cloned.1.call-update) | async-done | bytes 589840 | tf_op jit(solution)/shard_map/reduce_scatter | solution.py:331
  583.3 12.3 %all-reduce.19 = (bf16[96]{0:T(256)(128)(2,1)S(1)}, bf16[96]{0:T(256)(128)(2,1)S(1)}, bf16[96]{0:T(256)(128)(2,1)S(1)}, bf16[96]{0:T(256)(128)(2,1)S(1)}, bf16[9...) all-reduce(bf16[96]{0:T(256)(128)(2,1)S(1)} %dynamic-slice.9, ...), channel_id=1, replica_groups=mesh['dp'=4,'fsdp'=8] {'dp'}, use_global_device_ids=true, to_apply=%region_29.30 | all-reduce | flops 1152 | bytes 4608 | tf_op jit(solution)/shard_map/psum | solution.py:334
  609.4 56.2 %all-reduce.23.cloned.1.call-done = (bf16[96,768]{0,1:T(8,128)(2,1)}, bf16[96,768]{0,1:T(8,128)(2,1)}, bf16[96,768]{0,1:T(8,128)(2,1)}, bf16[96,768]{1,0:T(8,128...) async-done(((bf16[96,768]{0,1:T(8,128)(2,1)}, bf16[96,768]{0,1:T(8,128)(2,1)}, bf16[96,768]{0,1:T(8,128)(2,1)}, bf16[96,768]{1,0:T(8,128)(2,1)}, ...) | async-done | bytes 1769488 | tf_op jit(solution)/shard_map/psum | solution.py:334
  (399 shorter events, 117.9 us)
Async XLA Ops:
  7.2 53.9 %all-gather.10.cloned.1.call-start = ((), (), s32[]{:S(2)}) async-start(), calls=%async_computation.7 | async-start | bytes 1327104 | tf_op jit(solution)/shard_map/all_gather | solution.py:289
  7.9 60.1 %all-gather.8.cloned.1.call-start = ((), (), s32[]{:S(2)}) async-start(), calls=%async_computation.6 | async-start | bytes 1327104 | tf_op jit(solution)/shard_map/all_gather | solution.py:292
  8.7 79.8 %all-gather.12.cloned.1.call-start = ((), (), s32[]{:S(2)}) async-start(), calls=%async_computation.8 | async-start | bytes 1327104 | tf_op jit(solution)/shard_map/all_gather | solution.py:291
  9.4 104.7 %all-gather.14.cloned.1.call-start = ((), (), s32[]{:S(2)}) async-start(), calls=%async_computation.9 | async-start | bytes 1327104 | tf_op jit(solution)/shard_map/all_gather | solution.py:294
  10.0 144.7 %all-gather.16.cloned.1.call-start = ((), (), s32[]{:S(2)}) async-start(), calls=%async_computation.10 | async-start | bytes 5308416 | tf_op jit(solution)/shard_map/all_gather | solution.py:298
  10.6 187.0 %all-gather.18.cloned.1.call-start = ((), (), s32[]{:S(2)}) async-start(), calls=%async_computation.11 | async-start | bytes 5308416 | tf_op jit(solution)/shard_map/all_gather | solution.py:300
  11.1 403.1 %reduce-scatter.23.cloned.1.call-start = ((), (), s32[]{:S(2)}) async-start(), calls=%async_computation.17 | async-start | bytes 1327104
  50.6 200.3 %copy-start.78 = (f32[768]{0:T(1024)}, f32[768]{0:T(1024)S(1)}, u32[]{:S(2)}) copy-start(f32[768]{0:T(1024)S(1)} %convert_element_type.406) | copy-start | bytes 9220
  50.6 153.5 %copy-start.96 = (f32[768]{0:T(1024)}, f32[768]{0:T(1024)S(1)}, u32[]{:S(2)}) copy-start(f32[768]{0:T(1024)S(1)} %convert_element_type.407) | copy-start | bytes 9220
  61.0 62.8 %copy-start.18 = (pred[512,512]{0,1:T(8,128)(4,1)}, pred[512,512]{0,1:T(8,128)(4,1)S(1)}, u32[]{:S(2)}) copy-start(pred[512,512]{0,1:T(8,128)(4,1)S(1)} %compare_and_fusion) | copy-start | bytes 786436
  90.8 27.0 %copy-start.12 = (bf16[512,768]{0,1:T(8,128)(2,1)}, bf16[512,768]{0,1:T(8,128)(2,1)S(1)}, u32[]{:S(2)}) copy-start(bf16[512,768]{0,1:T(8,128)(2,1)S(1)} %copy.107) | copy-start | bytes 2359300
  116.7 134.3 %copy-start.66 = (f32[512]{0:T(512)}, f32[512]{0:T(512)S(1)}, u32[]{:S(2)}) copy-start(f32[512]{0:T(512)S(1)} %broadcast_multiply_fusion.3) | copy-start | bytes 6148
  117.0 134.0 %copy-start.90 = (f32[512]{0:T(512)}, f32[512]{0:T(512)S(1)}, u32[]{:S(2)}) copy-start(f32[512]{0:T(512)S(1)} %fusion.62) | copy-start | bytes 6148
  129.5 121.5 %copy-start.68 = (f32[512]{0:T(512)}, f32[512]{0:T(512)S(1)}, u32[]{:S(2)}) copy-start(f32[512]{0:T(512)S(1)} %broadcast_multiply_fusion.1) | copy-start | bytes 6148
  130.7 120.3 %copy-start.92 = (f32[512]{0:T(512)}, f32[512]{0:T(512)S(1)}, u32[]{:S(2)}) copy-start(f32[512]{0:T(512)S(1)} %fusion.64) | copy-start | bytes 6148
  130.7 31.9 %copy-start.28 = (f32[512,768]{1,0:T(8,128)S(1)}, f32[512,768]{1,0:T(8,128)}, u32[]{:S(2)}) copy-start(f32[512,768]{1,0:T(8,128)} %copy-done.27) | copy-start | bytes 4718596
  154.7 7.9 %copy-start.102 = (bf16[768,3072]{1,0:T(8,128)(2,1)S(1)}, bf16[768,3072]{1,0:T(8,128)(2,1)}, u32[]{:S(2)}) copy-start(bf16[768,3072]{1,0:T(8,128)(2,1)} %all-gather.16.cloned.1.call-done) | copy-start | bytes 14155780
  197.6 6.5 copy-start.31
  197.6 6.5 copy-start.103
  197.6 6.5 copy-start.109
  237.9 6.5 copy-start.29
  237.9 6.5 copy-start.32
  237.9 6.5 copy-start.112
  260.1 9.6 %copy-start.38 = (bf16[512,768]{0,1:T(8,128)(2,1)S(1)}, bf16[512,768]{0,1:T(8,128)(2,1)}, u32[]{:S(2)}) copy-start(bf16[512,768]{0,1:T(8,128)(2,1)} %copy.101) | copy-start | bytes 2359300
  260.1 9.6 %copy-start.39 = (bf16[512,768]{0,1:T(8,128)(2,1)S(1)}, bf16[512,768]{0,1:T(8,128)(2,1)}, u32[]{:S(2)}) copy-start(bf16[512,768]{0,1:T(8,128)(2,1)} %copy.109) | copy-start | bytes 2359300
  269.7 10.2 %copy-start.8 = (f32[512,768]{1,0:T(8,128)S(1)}, f32[512,768]{1,0:T(8,128)}, u32[]{:S(2)}) copy-start(f32[512,768]{1,0:T(8,128)} %get-tuple-element.144) | copy-start | bytes 4718596
  269.7 11.9 %copy-start.107 = (bf16[768,768]{1,0:T(8,128)(2,1)S(1)}, bf16[768,768]{1,0:T(8,128)(2,1)}, u32[]{:S(2)}) copy-start(bf16[768,768]{1,0:T(8,128)(2,1)} %all-gather.14.cloned.1.call-done) | copy-start | bytes 3538948
  285.5 8.7 %copy-start.37 = (bf16[512,768]{0,1:T(8,128)(2,1)S(1)}, bf16[512,768]{0,1:T(8,128)(2,1)}, u32[]{:S(2)}) copy-start(bf16[512,768]{0,1:T(8,128)(2,1)} %copy.105) | copy-start | bytes 2359300
  285.5 8.7 %copy-start.40 = (bf16[512,768]{0,1:T(8,128)(2,1)S(1)}, bf16[512,768]{0,1:T(8,128)(2,1)}, u32[]{:S(2)}) copy-start(bf16[512,768]{0,1:T(8,128)(2,1)} %copy.113) | copy-start | bytes 2359300
  294.3 10.7 %copy-start.41 = (bf16[12,64,512]{2,1,0:T(8,128)(2,1)}, bf16[12,64,512]{2,1,0:T(8,128)(2,1)S(1)}, u32[]{:S(2)}) copy-start(bf16[12,64,512]{2,1,0:T(8,128)(2,1)S(1)} %get-tuple-element.203) | copy-start | bytes 2359300
  294.3 9.9 %copy-start.5 = (bf16[1024,768]{1,0:T(8,128)(2,1)S(1)}, bf16[1024,768]{1,0:T(8,128)(2,1)}, u32[]{:S(2)}) copy-start(bf16[1024,768]{1,0:T(8,128)(2,1)} %param.19) | copy-start | bytes 4718596
  294.3 9.9 %copy-start.47 = (bf16[12,64,512]{2,1,0:T(8,128)(2,1)S(1)}, bf16[12,64,512]{2,1,0:T(8,128)(2,1)}, u32[]{:S(2)}) copy-start(bf16[12,64,512]{2,1,0:T(8,128)(2,1)} %get-tuple-element.201) | copy-start | bytes 2359300
  309.2 106.9 %reduce-scatter.21.cloned.1.call-start = ((), (), s32[]{:S(2)}) async-start(), calls=%async_computation.16 | async-start | bytes 1327104
  309.3 16.4 %slice-start = ((s8[12582912]{0:T(1024)(128)(4,1)}), s8[4194304]{0:T(1024)(128)(4,1)S(1)}, s32[]{:S(2)}) async-start(s8[12582912]{0:T(1024)(128)(4,1)} %bitcast.126), calls=%async_computation.19 | async-start | bytes 8388608
  309.3 10.9 %copy-start.17 = (bf16[512,768]{0,1:T(8,128)(2,1)S(1)}, bf16[512,768]{0,1:T(8,128)(2,1)}, u32[]{:S(2)}) copy-start(bf16[512,768]{0,1:T(8,128)(2,1)} %copy.102) | copy-start | bytes 2359300
  309.3 16.4 %slice-start.1 = ((s8[12582912]{0:T(1024)(128)(4,1)}), s8[4194304]{0:T(1024)(128)(4,1)S(1)}, s32[]{:S(2)}) async-start(s8[12582912]{0:T(1024)(128)(4,1)} %bitcast.126), calls=%async_computation.20 | async-start | bytes 8388608
  309.3 16.4 %slice-start.2 = ((s8[12582912]{0:T(1024)(128)(4,1)}), s8[4194304]{0:T(1024)(128)(4,1)S(1)}, s32[]{:S(2)}) async-start(s8[12582912]{0:T(1024)(128)(4,1)} %bitcast.126), calls=%async_computation.21 | async-start | bytes 8388608
  325.7 7.1 %copy-start.16 = (bf16[512,768]{0,1:T(8,128)(2,1)S(1)}, bf16[512,768]{0,1:T(8,128)(2,1)}, u32[]{:S(2)}) copy-start(bf16[512,768]{0,1:T(8,128)(2,1)} %copy.106) | copy-start | bytes 2359300
  340.5 86.0 %reduce-scatter.19.cloned.1.call-start = ((), (), s32[]{:S(2)}) async-start(), calls=%async_computation.15 | async-start | bytes 1327104
  356.0 110.9 %reduce-scatter.13.cloned.1.call-start = ((), (), s32[]{:S(2)}) async-start(), calls=%async_computation.12 | async-start | bytes 1327104 | tf_op jit(solution)/shard_map/reduce_scatter | solution.py:331
  360.3 163.9 %reduce-scatter.17.cloned.1.call-start = ((), (), s32[]{:S(2)}) async-start(), calls=%async_computation.14 | async-start | bytes 5308416 | tf_op jit(solution)/shard_map/reduce_scatter | solution.py:331
  370.0 211.3 %reduce-scatter.15.cloned.1.call-start = ((), (), s32[]{:S(2)}) async-start(), calls=%async_computation.13 | async-start | bytes 5308416 | tf_op jit(solution)/shard_map/reduce_scatter | solution.py:331
  381.1 284.5 %all-reduce.23.cloned.1.call-start = ((), (), s32[]{:S(2)}) async-start(), calls=%async_computation.18 | async-start | bytes 3833856 | tf_op jit(solution)/shard_map/psum | solution.py:334
  414.3 167.1 %copy-start.45 = (bf16[512,768]{1,0:T(8,128)(2,1)S(1)}, bf16[512,768]{1,0:T(8,128)(2,1)}, u32[]{:S(2)}) copy-start(bf16[512,768]{1,0:T(8,128)(2,1)} %get-tuple-element.165) | copy-start | bytes 2359300
  414.3 167.1 %copy-start.46 = (bf16[512,768]{1,0:T(8,128)(2,1)S(1)}, bf16[512,768]{1,0:T(8,128)(2,1)}, u32[]{:S(2)}) copy-start(bf16[512,768]{1,0:T(8,128)(2,1)} %get-tuple-element.166) | copy-start | bytes 2359300
  414.3 186.0 %copy-start.51 = (bf16[12,64,512]{2,1,0:T(8,128)(2,1)S(1)}, bf16[12,64,512]{2,1,0:T(8,128)(2,1)}, u32[]{:S(2)}) copy-start(bf16[12,64,512]{2,1,0:T(8,128)(2,1)} %copy-done.50) | copy-start | bytes 2359300
  581.3 21.2 %copy-start.23 = (bf16[12,64,512]{2,1,0:T(8,128)(2,1)S(1)}, bf16[12,64,512]{2,1,0:T(8,128)(2,1)}, u32[]{:S(2)}) copy-start(bf16[12,64,512]{2,1,0:T(8,128)(2,1)} %copy-done.22) | copy-start | bytes 2359300
  665.6 9.2 %copy-start.60 = (bf16[384,768]{1,0:T(8,128)(2,1)S(1)}, bf16[384,768]{1,0:T(8,128)(2,1)}, u32[]{:S(2)}) copy-start(bf16[384,768]{1,0:T(8,128)(2,1)} %get-tuple-element.130) | copy-start | bytes 1769476
  (82 other events, 248.7 us)
Sparse Core Ops, SparseCore 0:
  9.9 26.7 all-gather.9
  38.6 23.9 all-gather.7
  64.5 23.9 all-gather.11
  90.2 23.9 all-gather.13
  115.9 38.7 all-gather.15
  156.4 38.7 all-gather.17
  309.4 36.6 reduce-scatter.22
  349.3 36.6 reduce-scatter.20
  389.8 36.6 reduce-scatter.18
  430.2 36.6 reduce-scatter.12
  470.4 53.7 reduce-scatter.16
  527.5 53.7 reduce-scatter.14
  584.7 80.7 all-reduce.22
where the time goes:
time: 687 us; the launch traced here: 683 us
  waiting for transfers between devices  261 us (38%)
  matrix products  216 us (31%)
  blocking collectives  70.4 us (10%)
  local copies, waits for them, and re-layouts  59.3 us (9%)
  other arithmetic  55.7 us (8%)
  between operations  18.9 us (3%)
    reduce_scatter x3, waiting for transfers between devices, on_device(): lax.psum_scatter(for_sending(summed_full), 'fsdp', scatter_dimension=0, t...  153 us
    dot_general x10, matrix products, project(): jnp.dot(inputs_low, matrix, preferred_element_type=jnp.float32)  62 us
    psum x1, waiting for transfers between devices, on_device(): lax.psum(for_sending(owned_sums), 'dp')  56.2 us
    unnamed x2, blocking collectives  49.6 us
    unnamed x270, local copies, waits for them, and re-layouts  43.9 us
    all_gather x1, waiting for transfers between devices, on_device(): lax.all_gather(shards[9], 'fsdp', axis=0, tiled=True)  24 us
    dot_general x2, matrix products, backward(): jnp.einsum('td,fd->tf', d_down, w_down, preferred_element_type=jnp.float32)  23.2 us
    dot_general x2, matrix products, backward(): jnp.einsum('qhd,khd->hqk', d_context, value_low, preferred_element_type=j...  19.5 us
  transfers between devices with their start and end apart: 13, of which 8 were waited for; matrix products, arithmetic and copies ran while one was open for 29% of the time, Pallas kernels for 0%

commit v1 on v0

--- a/solution.py
+++ b/solution.py
@@ -1,3 +1,5 @@
+import functools
+
 import jax
 import jax.numpy as jnp
 from jax import lax
@@ -233,106 +235,147 @@
     return (d_tokens, gradients)
 
 
-def on_device(
-    tokens,
-    cotangent,
-    bucket,
-    lengths,
-    w_query,
-    b_query,
-    w_key,
-    w_value,
-    b_value,
-    w_out,
-    b_out,
-    gain_one,
-    shift_one,
-    w_up,
-    b_up,
-    w_down,
-    b_down,
-    gain_two,
-    shift_two,
-):
-    shards = (
-        w_query,
-        b_query,
-        w_key,
-        w_value,
-        b_value,
-        w_out,
-        b_out,
-        gain_one,
-        shift_one,
-        w_up,
-        b_up,
-        w_down,
-        b_down,
-        gain_two,
-        shift_two,
-    )
+def bits_of(count):
+    bits = [1 << i for i in range(count.bit_length() - 1)]
+    assert count == 1 << len(bits), "axis size"
+    return bits
+
+
+def swap(x, bit, axis, count):
+    return lax.ppermute(x, axis, [(i, i ^ bit) for i in range(count)])
+
+
+def gather_rel(x, order, count):
+    pieces = {0: x}
+    for bit in order:
+        pieces.update({m | bit: swap(p, bit, "fsdp", count) for m, p in list(pieces.items())})
+    return pieces
+
+
+def place(pieces, me):
+    rows = pieces[0].shape[0]
+    whole = jnp.zeros((rows * len(pieces), pieces[0].shape[1]), pieces[0].dtype)
+    for m, piece in pieces.items():
+        whole = lax.dynamic_update_slice_in_dim(whole, piece, (me ^ m) * rows, axis=0)
+    return whole
+
+
+def add_low(a, b):
+    return (a.astype(jnp.float32) + b.astype(jnp.float32)).astype(jnp.bfloat16)
+
+
+def reduce_rel(parts, order, count):
+    for bit in order:
+        sent = [m for m in sorted(parts) if m & bit]
+        got = swap(jnp.concatenate([parts[m] for m in sent], axis=0), bit, "fsdp", count)
+        got = jnp.split(got, len(sent), axis=0)
+        parts = {m ^ bit: add_low(parts[m ^ bit], g) for m, g in zip(sent, got)}
+    return parts[0]
+
+
+def sum_over_dp(x, count):
+    at = lax.axis_index("dp")
+    bits = bits_of(count)
+    for bit in bits:
+        low, high = jnp.split(x, 2, axis=0)
+        upper = (at & bit) != 0
+        got = swap(jnp.where(upper, low, high), bit, "dp", count)
+        x = add_low(jnp.where(upper, high, low), got)
+    for bit in reversed(bits):
+        upper = (at & bit) != 0
+        got = swap(x, bit, "dp", count)
+        x = jnp.concatenate([jnp.where(upper, got, x), jnp.where(upper, x, got)], axis=0)
+    return x
+
+
+VECTORS = (1, 4, 6, 7, 8, 10, 12, 13, 14)
+
+
+def pack_vectors(vecs, shard):
+    return jnp.concatenate([v.reshape(-1, shard) for v in vecs], axis=0)
+
+
+def on_device(sizes, tokens, cotangent, bucket, lengths, *shards):
+    dp, fsdp = sizes
+    me = lax.axis_index("fsdp")
+    chip_bits = bits_of(fsdp)[1:]
+    up, down = chip_bits + [1], chip_bits[::-1] + [1]
+    model = tokens.shape[1]
+    shard = shards[0].shape[0]
     micro_count = bucket.shape[0]
     slot_count = tokens.shape[0] // micro_count
-    summed_full = None
-    owned_sums = None
+
+    vecs = pack_vectors([shards[i] for i in VECTORS], shard)
+    half = shard // 2
+    first = jnp.concatenate([shards[0], shards[2][:half]], axis=0)
+    second = jnp.concatenate([shards[3], shards[2][half:]], axis=0)
+    got_v = gather_rel(vecs, down, fsdp)
+    got_1, got_2 = gather_rel(first, up, fsdp), gather_rel(second, down, fsdp)
+    got_o1, got_o2 = gather_rel(shards[5][:half], up, fsdp), gather_rel(shards[5][half:], down, fsdp)
+    got_up, got_down = gather_rel(shards[9], up, fsdp), gather_rel(shards[11], down, fsdp)
+
+    weights = [None] * 15
+    weights[0] = place({m: p[:shard] for m, p in got_1.items()}, me)
+    weights[3] = place({m: p[:shard] for m, p in got_2.items()}, me)
+    weights[2] = place(
+        {m: jnp.concatenate([p[shard:], got_2[m][shard:]], axis=0) for m, p in got_1.items()}, me
+    )
+    weights[5] = place(
+        {m: jnp.concatenate([p, got_o2[m]], axis=0) for m, p in got_o1.items()}, me
+    )
+    weights[9] = place(got_up, me)
+    weights[11] = place(got_down, me)
+    rows = vecs.shape[0]
+    all_vecs = place(got_v, me).reshape(fsdp, rows, shard)
+    at = 0
+    for i in VECTORS:
+        n = shards[i].shape[0] // shard
+        weights[i] = all_vecs[:, at : at + n].reshape(-1)
+        at += n
+    weights = tuple(weights)
+
+    summed = None
     outputs = []
     token_grads = []
-    for micro_idx in range(micro_count):
-        tok_rows = lax.slice_in_dim(
-            tokens, micro_idx * slot_count, (micro_idx + 1) * slot_count, axis=0
-        )
-        cot_rows = lax.slice_in_dim(
-            cotangent, micro_idx * slot_count, (micro_idx + 1) * slot_count, axis=0
-        )
-        allowed, live_rows = key_mask(bucket[micro_idx], lengths[micro_idx], slot_count)
-        fwd_weights = (
-            lax.all_gather(shards[0], "fsdp", axis=0, tiled=True),
-            lax.all_gather(shards[1], "fsdp", axis=0, tiled=True),
-            lax.all_gather(shards[2], "fsdp", axis=0, tiled=True),
-            lax.all_gather(shards[3], "fsdp", axis=0, tiled=True),
-            lax.all_gather(shards[4], "fsdp", axis=0, tiled=True),
-            lax.all_gather(shards[5], "fsdp", axis=0, tiled=True),
-            lax.all_gather(shards[6], "fsdp", axis=0, tiled=True),
-            lax.all_gather(shards[7], "fsdp", axis=0, tiled=True),
-            lax.all_gather(shards[8], "fsdp", axis=0, tiled=True),
-            lax.all_gather(shards[9], "fsdp", axis=0, tiled=True),
-            lax.all_gather(shards[10], "fsdp", axis=0, tiled=True),
-            lax.all_gather(shards[11], "fsdp", axis=0, tiled=True),
-            lax.all_gather(shards[12], "fsdp", axis=0, tiled=True),
-            lax.all_gather(shards[13], "fsdp", axis=0, tiled=True),
-            lax.all_gather(shards[14], "fsdp", axis=0, tiled=True),
-        )
-        output, kept = forward(fwd_weights, tok_rows, allowed)
+    for i in range(micro_count):
+        tok_rows = lax.slice_in_dim(tokens, i * slot_count, (i + 1) * slot_count, axis=0)
+        cot_rows = lax.slice_in_dim(cotangent, i * slot_count, (i + 1) * slot_count, axis=0)
+        allowed, live_rows = key_mask(bucket[i], lengths[i], slot_count)
+        output, kept = forward(weights, tok_rows, allowed)
         outputs.append(output)
-        back_weights = (
-            lax.all_gather(shards[0], "fsdp", axis=0, tiled=True),
-            lax.all_gather(shards[1], "fsdp", axis=0, tiled=True),
-            lax.all_gather(shards[2], "fsdp", axis=0, tiled=True),
-            lax.all_gather(shards[3], "fsdp", axis=0, tiled=True),
-            lax.all_gather(shards[4], "fsdp", axis=0, tiled=True),
-            lax.all_gather(shards[5], "fsdp", axis=0, tiled=True),
-            lax.all_gather(shards[6], "fsdp", axis=0, tiled=True),
-            lax.all_gather(shards[7], "fsdp", axis=0, tiled=True),
-            lax.all_gather(shards[8], "fsdp", axis=0, tiled=True),
-            lax.all_gather(shards[9], "fsdp", axis=0, tiled=True),
-            lax.all_gather(shards[10], "fsdp", axis=0, tiled=True),
-            lax.all_gather(shards[11], "fsdp", axis=0, tiled=True),
-            lax.all_gather(shards[12], "fsdp", axis=0, tiled=True),
-            lax.all_gather(shards[13], "fsdp", axis=0, tiled=True),
-            lax.all_gather(shards[14], "fsdp", axis=0, tiled=True),
-        )
-        d_tokens, gradients = backward(back_weights, tok_rows, allowed, live_rows, cot_rows, kept)
+        d_tokens, gradients = backward(weights, tok_rows, allowed, live_rows, cot_rows, kept)
         token_grads.append(d_tokens)
-        summed_full = (
-            gradients if summed_full is None else jax.tree.map(jnp.add, summed_full, gradients)
-        )
-    owned_sums = jax.tree.map(
-        lambda part: part.astype(jnp.float32),
-        lax.psum_scatter(for_sending(summed_full), "fsdp", scatter_dimension=0, tiled=True),
-    )
-    finals = jax.tree.map(
-        lambda part: part.astype(jnp.float32), lax.psum(for_sending(owned_sums), "dp")
-    )
+        summed = gradients if summed is None else jax.tree.map(jnp.add, summed, gradients)
+
+    def relative(whole):
+        n = whole.shape[0] // fsdp
+        return {
+            m: lax.dynamic_slice_in_dim(whole, (me ^ m) * n, n, axis=0).astype(jnp.bfloat16)
+            for m in range(fsdp)
+        }
+
+    core_first_up, core_first_down = [1] + chip_bits, [1] + chip_bits[::-1]
+
+    def reduced(whole, order):
+        return sum_over_dp(reduce_rel(relative(whole), order, fsdp), dp).astype(jnp.float32)
+
+    finals = [None] * 15
+    finals[11] = reduced(summed[11], core_first_down)
+    finals[9] = reduced(summed[9], core_first_up)
+    finals[5] = reduced(summed[5], core_first_up)
+    for i, order in ((0, core_first_up), (2, core_first_down), (3, core_first_up)):
+        finals[i] = reduced(summed[i], order)
+    by_shard = jnp.concatenate(
+        [summed[i].reshape(fsdp, -1, shard) for i in VECTORS], axis=1
+    )
+    pad = (-rows) % (2 * dp)
+    by_shard = jnp.pad(by_shard, ((0, 0), (0, pad), (0, 0)))
+    small = reduced(by_shard.reshape(fsdp * (rows + pad), shard), core_first_down)
+    at = 0
+    for i in VECTORS:
+        n = shards[i].shape[0] // shard
+        finals[i] = small[at : at + n].reshape(-1)
+        at += n
     return (jnp.concatenate(outputs, axis=0), jnp.concatenate(token_grads, axis=0)) + tuple(finals)
 
 
@@ -358,8 +401,9 @@
         P("fsdp"),
         P("fsdp"),
     )
+    sizes = (mesh.shape["dp"], mesh.shape["fsdp"])
     return jax.shard_map(
-        on_device,
+        functools.partial(on_device, sizes),
         mesh=mesh,
         in_specs=placed,
         out_specs=(

time: 687 us -> 576 us (0.84)
  waiting for transfers between devices: 261 us -> 128 us
  starting transfers between devices: 1.09 us -> 76.4 us
  blocking collectives: 70.4 us -> 0 us
  other arithmetic: 55.7 us -> 77.1 us
  between operations: 18.9 us -> 4.62 us
  local copies, waits for them, and re-layouts: 59.3 us -> 69 us
    reduce_scatter x3 -> x0, waiting for transfers between devices: 153 us -> none  [on_device(): lax.psum_scatter(for_sending(summed_full), 'fsdp', scatter_dimension=0, t...]
    ppermute x0 -> x98, waiting for transfers between devices: none -> 128 us  [swap(): return lax.ppermute(x, axis, [(i, i ^ bit) for i in range(count)])]
    ppermute x0 -> x98, starting transfers between devices: none -> 76.4 us  [swap(): return lax.ppermute(x, axis, [(i, i ^ bit) for i in range(count)])]
    psum x1 -> x0, waiting for transfers between devices: 56.2 us -> none  [on_device(): lax.psum(for_sending(owned_sums), 'dp')]
    unnamed x2 -> x0, blocking collectives: 49.6 us -> none
    all_gather x6 -> x0, waiting for transfers between devices: 39.9 us -> none  [the longest x1 24 us: on_device(): lax.all_gather(shards[9], 'fsdp', axis=0, tiled=True)]
    dynamic_update_slice x0 -> x42, local copies, waits for them, and re-layouts: none -> 31.5 us  [place(): lax.dynamic_update_slice_in_dim(whole, piece, (me ^ m) * rows, axis=0)]
    unnamed x270 -> x234, local copies, waits for them, and re-layouts: 43.9 us -> 16.9 us
  transfers between devices with their start and end apart: 13 -> 98, of which waited for: 8 -> 40; matrix products, arithmetic and copies ran while one was open for 29% -> 33% of each run, Pallas kernels for 0% -> 0%
where the time goes in v1:
time: 576 us; the launch traced here: 568 us
  matrix products  212 us (37%)
  waiting for transfers between devices  128 us (22%)
  other arithmetic  77.1 us (13%)
  starting transfers between devices  76.4 us (13%)
  local copies, waits for them, and re-layouts  69 us (12%)
    ppermute x98, waiting for transfers between devices, swap(): return lax.ppermute(x, axis, [(i, i ^ bit) for i in range(count)])  128 us
    ppermute x98, starting transfers between devices, swap(): return lax.ppermute(x, axis, [(i, i ^ bit) for i in range(count)])  76.4 us
    dot_general x10, matrix products, project(): jnp.dot(inputs_low, matrix, preferred_element_type=jnp.float32)  63.6 us
    dynamic_update_slice x42, local copies, waits for them, and re-layouts, place(): lax.dynamic_update_slice_in_dim(whole, piece, (me ^ m) * rows, axis=0)  31.5 us
    dot_general x2, matrix products, backward(): jnp.einsum('td,fd->tf', d_down, w_down, preferred_element_type=jnp.float32)  25.9 us
    dot_general x2, matrix products, backward(): jnp.einsum('qhd,khd->hqk', d_context, value_low, preferred_element_type=j...  20.5 us
    convert_element_type x35, other arithmetic, add_low(): return (a.astype(jnp.float32) + b.astype(jnp.float32)).astype(jnp.bfloat16)  19.2 us
    unnamed x234, local copies, waits for them, and re-layouts  16.9 us
  transfers between devices with their start and end apart: 98, of which 40 were waited for; matrix products, arithmetic and copies ran while one was open for 33% of the time, Pallas kernels for 0%

profile of v1, /device:TPU:0, one launch (start us, length us, event | category | flops | bytes accessed | tf_op | source)
XLA Modules:
  0.0 567.5 jit_solution(2578116174698530154)
XLA Ops:
  3.0 3.0 collective-permute-start.7
  19.4 2.8 broadcast_in_dim.135
  58.6 3.5 collective-permute-done.1
  63.6 4.4 collective-permute-done.15
  72.3 9.6 %collective-permute-done.2 = bf16[144,768]{1,0:T(8,128)(2,1)S(1)} collective-permute-done((bf16[144,768]{1,0:T(8,128)(2,1)S(1)}, bf16[144,768]{1,0:T(8,128)(2,1)S(1)}, u32[]{:S(2)}, u32[]{:S(2)}) %collective-permute-start.2) | collective-permute-done | bytes 221216 | tf_op jit(solution)/shard_map/ppermute | solution.py:245
  91.4 8.3 %collective-permute-done.42 = bf16[384,768]{1,0:T(8,128)(2,1)S(1)} collective-permute-done((bf16[384,768]{1,0:T(8,128)(2,1)}, bf16[384,768]{1,0:T(8,128)(2,1)S(1)}, u32[]{:S(2)}, u32[]{:S(2)}) %collective-permute-start.42) | collective-permute-done | bytes 589856 | tf_op jit(solution)/shard_map/ppermute | solution.py:245
  113.2 3.3 add_convert_fusion.3
  122.1 3.1 fusion
  126.7 3.6 fusion.37
  141.4 3.7 fusion.36
  153.7 10.8 %collective-permute-done.44 = bf16[384,768]{1,0:T(8,128)(2,1)S(1)} collective-permute-done((bf16[384,768]{1,0:T(8,128)(2,1)S(1)}, bf16[384,768]{1,0:T(8,128)(2,1)S(1)}, u32[]{:S(2)}, u32[]{:S(2)}) %collective-permute-start.44) | collective-permute-done | bytes 589856 | tf_op jit(solution)/shard_map/ppermute | solution.py:245
  174.3 4.8 fusion.112
  179.2 34.4 %multiply_convert_fusion.3 = (bf16[512,3072]{1,0:T(8,128)(2,1)S(1)}, f32[512,3072]{1,0:T(8,128)}, bf16[512,3072]{1,0:T(8,128)(2,1)S(1)}, f32[512,3072]{1,0:T(8,128)}, f32[512,3072]{1,0:T(8,128)}) fusion(f32[3072]{0:T(1024)S(1)} %reshape.733, f32[512,3072]{1,0:T(8,128)S(1)} %fusion.112, bf16[768,3072]{1,0:T(8,128)(2,1)} %constant_dynamic-update-slice_fusion.8, ...), kind=kOutput, calls=%fused_computation.41 | convolution fusion | flops 2625503232 | bytes 37771264 | tf_op jit(solution)/shard_map/dot_general | solution.py:45
  214.6 5.4 fusion.132
  220.3 5.2 fusion.131
  229.2 2.7 fusion.121
  232.1 5.1 fusion.139
  237.4 7.2 %fusion.135 = f32[512,3072]{1,0:T(8,128)} fusion(bf16[512,768]{1,0:T(8,128)(2,1)S(1)} %get-tuple-element.40, bf16[3072,768]{1,0:T(8,128)(2,1)} %constant_dynamic-update-slice_fusion), kind=kOutput, calls=%fused_computation.510 | convolution fusion | flops 2415919104 | bytes 11796480 | tf_op jit(solution)/shard_map/td,fd->tf/dot_general | solution.py:162
  244.5 18.8 %convert_reduce_fusion.1 = (f32[3072]{0:T(1024)}, bf16[512,3072]{1,0:T(8,128)(2,1)}, f32[3072]{0:T(1024)}, bf16[512,3072]{1,0:T(8,128)(2,1)}) fusion(f32[512,3072]{1,0:T(8,128)} %get-tuple-element.64, f32[512,3072]{1,0:T(8,128)} %get-tuple-element.175, f32[3072]{0:T(1024)S(1)} %reshape.733, f32[512,3072]{1,0:T(8,128)} %fusion.135, ...), kind=kOutput, calls=%fused_computation.23 | convolution fusion | flops 2469390336 | bytes 43290624 | tf_op jit(solution)/shard_map/td,fd->tf/dot_general | solution.py:162
  263.3 6.1 %add_add_fusion.10 = f32[512,768]{1,0:T(8,128)S(1)} fusion(f32[512,768]{1,0:T(8,128)S(1)} %get-tuple-element.58, bf16[512,3072]{1,0:T(8,128)(2,1)} %get-tuple-element.143, bf16[768,3072]{1,0:T(8,128)(2,1)} %constant_dynamic-update-slice_fusion.8, f32[512]{0:T(512)S(1)} %negate_multiply_fusion.3), kind=kOutput, calls=%fused_computation.119 | convolution fusion | flops 2416705536 | bytes 11012096 | tf_op jit(solution)/shard_map/tf,df->td/dot_general | solution.py:167
  269.4 6.4 %multiply_reduce_fusion.5 = (f32[768]{0:T(1024)}, f32[512]{0:T(512)S(1)}, f32[768]{0:T(1024)}, f32[768]{0:T(1024)}, f32[512]{0:T(512)S(1)}, /*index=5*/f32[768]{0:T(1024)}, f32[512,768]{1,0:T(8,128)S(1)}) fusion(f32[512,768]{1,0:T(8,128)S(1)} %copy-done.24, f32[512]{0:T(512)S(1)} %fusion.99, f32[512]{0:T(512)S(1)} %broadcast_multiply_fusion.3, ...), kind=kOutput, calls=%fused_computation.79 | convolution fusion | flops 2422992896 | bytes 15758336 | tf_op jit(solution)/shard_map/tf,df->td/dot_general | solution.py:167
  283.1 7.5 %convert_reduce_fusion.7 = (f32[12,64]{1,0:T(8,128)S(1)}, bf16[12,64,512]{2,1,0:T(8,128)(2,1)}) fusion(bf16[512,12,64]{0,2,1:T(8,128)(2,1)S(1)} %bitcast.249, f32[12,512]{1,0:T(8,128)S(1)} %copy-done.73, f32[12,512,512]{1,2,0:T(8,128)} %copy-done, pred[512,512]{0,1:T(8,128)(4,1)S(1)} %copy-done.14), kind=kOutput, calls=%fused_computation.83 | convolution fusion | flops 416414976 | bytes 14445568 | tf_op jit(solution)/shard_map/hqk,qhd->khd/dot_general | solution.py:181
  290.6 9.6 %multiply_reduce_fusion.1 = (f32[12,512]{1,0:T(8,128)S(1)}, f32[12,512,512]{1,2,0:T(8,128)}) fusion(f32[12,512]{1,0:T(8,128)S(1)} %copy-done.73, f32[12,512,512]{1,2,0:T(8,128)} %copy-done, pred[512,512]{0,1:T(8,128)(4,1)S(1)} %copy-done.14, bf16[512,12,64]{0,2,1:T(8,128)(2,1)S(1)} %bitcast.250, bf16[512,12,64]{0,2,1:T(8,128)(2,1)S(1)} %bitcast.268), kind=kOutput, calls=%fused_computation.4 | convolution fusion | flops 418375680 | bytes 27049984 | tf_op jit(solution)/shard_map/qhd,khd->hqk/dot_general | solution.py:190
  303.7 7.4 %convert_reduce_fusion.6 = (f32[12,64]{1,0:T(8,128)S(1)}, bf16[12,64,512]{2,1,0:T(8,128)(2,1)}) fusion(bf16[512,12,64]{0,2,1:T(8,128)(2,1)S(1)} %bitcast.251, f32[12,512]{1,0:T(8,128)S(1)} %copy-done.74, f32[12,512,512]{1,2,0:T(8,128)} %copy-done.1, pred[512,512]{0,1:T(8,128)(4,1)S(1)} %copy-done.16), kind=kOutput, calls=%fused_computation.82 | convolution fusion | flops 416414976 | bytes 14445568 | tf_op jit(solution)/shard_map/hqk,qhd->khd/dot_general | solution.py:181
  311.2 11.0 %multiply_reduce_fusion = (f32[12,512]{1,0:T(8,128)S(1)}, f32[12,512,512]{1,2,0:T(8,128)}) fusion(f32[12,512]{1,0:T(8,128)S(1)} %copy-done.74, f32[12,512,512]{1,2,0:T(8,128)} %copy-done.1, pred[512,512]{0,1:T(8,128)(4,1)S(1)} %copy-done.16, bf16[512,12,64]{0,2,1:T(8,128)(2,1)S(1)} %bitcast.252, bf16[512,12,64]{0,2,1:T(8,128)(2,1)S(1)} %bitcast.266), kind=kOutput, calls=%fused_computation.1 | convolution fusion | flops 418375680 | bytes 27049984 | tf_op jit(solution)/shard_map/qhd,khd->hqk/dot_general | solution.py:190
  322.2 5.5 fusion.114
  330.0 8.1 %multiply_convert_fusion.1 = bf16[12,512,512]{1,2,0:T(8,128)(2,1)S(1)} fusion(f32[12,512,512]{1,2,0:T(8,128)} %get-tuple-element.184, f32[12,512]{1,0:T(8,128)S(1)} %get-tuple-element.183, f32[12,512]{1,0:T(8,128)S(1)} %copy-done.73, f32[12,512,512]{1,2,0:T(8,128)S(1)} %bitcast.236, pred[512,512]{0,1:T(8,128)(4,1)S(1)} %copy-done.14), kind=kLoop, calls=%fused_computation.3 | loop fusion | flops 18874368 | bytes 31768576 | tf_op jit(solution)/shard_map/convert_element_type | solution.py:193
  340.6 2.9 multiply_convert_fusion.6
  343.5 7.1 %multiply_convert_fusion = bf16[12,512,512]{1,2,0:T(8,128)(2,1)S(1)} fusion(f32[12,512,512]{1,2,0:T(8,128)} %get-tuple-element.182, f32[12,512]{1,0:T(8,128)S(1)} %get-tuple-element.181, f32[12,512]{1,0:T(8,128)S(1)} %copy-done.74, f32[12,512,512]{1,2,0:T(8,128)S(1)} %bitcast.238, pred[512,512]{0,1:T(8,128)(4,1)S(1)} %copy-done.16), kind=kLoop, calls=%fused_computation | loop fusion | flops 18874368 | bytes 31768576 | tf_op jit(solution)/shard_map/convert_element_type | solution.py:193
  351.8 2.9 multiply_convert_fusion.4
  357.0 3.3 fusion.133
  364.5 5.3 convolution_add_fusion
  375.8 8.0 %convolution_add_fusion.1 = bf16[768,3072]{1,0:T(8,128)(2,1)S(1)} fusion(f32[768,3072]{1,0:T(8,128)} %fusion.114, bf16[512,3072]{1,0:T(8,128)(2,1)} %get-tuple-element.143, f32[512,768]{1,0:T(8,128)} %copy-done.21, f32[512]{0:T(512)S(1)} %copy-done.88, f32[512]{0:T(512)S(1)} %broadcast_multiply_fusion.1, f32[768]{0:T(1024)S(1)} %copy-done.93, ...), kind=kOutput, calls=%fused_computation.59 | convolution fusion | flops 2422603776 | bytes 18884608 | tf_op jit(solution)/shard_map/td,tf->df/dot_general | solution.py:166
  397.9 2.6 fusion.136
  415.7 2.8 collective-permute-start.60
  420.4 2.6 collective-permute-start.61
  436.6 4.8 collective-permute-done.78
  443.1 4.6 collective-permute-done.71
  463.4 2.6 collective-permute-start.81
  493.7 15.7 %collective-permute-done.92 = bf16[768,768]{1,0:T(8,128)(2,1)S(1)} collective-permute-done((bf16[768,768]{1,0:T(8,128)(2,1)S(1)}, bf16[768,768]{1,0:T(8,128)(2,1)S(1)}, u32[]{:S(2)}, u32[]{:S(2)}) %collective-permute-start.92) | collective-permute-done | bytes 1179680 | tf_op jit(solution)/shard_map/ppermute | solution.py:245
  512.1 6.6 %collective-permute-done.85 = bf16[192,3072]{1,0:T(8,128)(2,1)S(1)} collective-permute-done((bf16[192,3072]{1,0:T(8,128)(2,1)S(1)}, bf16[192,3072]{1,0:T(8,128)(2,1)S(1)}, u32[]{:S(2)}, u32[]{:S(2)}) %collective-permute-start.85) | collective-permute-done | bytes 1179680 | tf_op jit(solution)/shard_map/ppermute | solution.py:245
  520.8 4.6 collective-permute-done.93
  531.6 5.4 collective-permute-done.94
  537.2 5.1 collective-permute-done.87
  542.5 5.5 collective-permute-done.95
  548.1 3.1 collective-permute-done.88
  551.4 4.2 collective-permute-done.96
  560.2 2.7 collective-permute-done.97
  (694 shorter events, 259.4 us)
Async XLA Ops:
  3.0 25.5 %collective-permute-start.7 = (bf16[12,96]{1,0:T(8,128)(2,1)S(1)}, bf16[12,96]{1,0:T(8,128)(2,1)S(1)}, u32[]{:S(2)}, u32[]{:S(2)}) collective-permute-start(bf16[12,96]{1,0:T(8,128)(2,1)S(1)} %concatenate.147), channel_id=1, source_target_pairs={{0,4},{1,5},{2,6},{3,7},{4,0},{5,1},{6,2},{7,3},{8,12},{9,13},{10,... | collective-permute-start | bytes 6920 | tf_op jit(solution)/shard_map/ppermute | solution.py:245
  6.0 23.9 %collective-permute-start.8 = (bf16[12,96]{1,0:T(8,128)(2,1)S(1)}, bf16[12,96]{1,0:T(8,128)(2,1)S(1)}, u32[]{:S(2)}, u32[]{:S(2)}) collective-permute-start(bf16[12,96]{1,0:T(8,128)(2,1)S(1)} %concatenate.147), channel_id=1, source_target_pairs={{0,2},{1,3},{2,0},{3,1},{4,6},{5,7},{6,4},{7,5},{8,10},{9,11},{10,... | collective-permute-start | bytes 6920 | tf_op jit(solution)/shard_map/ppermute | solution.py:245
  7.5 25.4 %collective-permute-start.10 = (bf16[12,96]{1,0:T(8,128)(2,1)S(1)}, bf16[12,96]{1,0:T(8,128)(2,1)S(1)}, u32[]{:S(2)}, u32[]{:S(2)}) collective-permute-start(bf16[12,96]{1,0:T(8,128)(2,1)S(1)} %concatenate.147), channel_id=1, source_target_pairs={{0,1},{1,0},{2,3},{3,2},{4,5},{5,4},{6,7},{7,6},{8,9},{9,8},{10,11... | collective-permute-start | bytes 6920 | tf_op jit(solution)/shard_map/ppermute | solution.py:245
  9.1 33.2 %collective-permute-start.22 = (bf16[48,768]{1,0:T(8,128)(2,1)S(1)}, bf16[48,768]{1,0:T(8,128)(2,1)S(1)}, u32[]{:S(2)}, u32[]{:S(2)}) collective-permute-start(bf16[48,768]{1,0:T(8,128)(2,1)S(1)} %get-tuple-element.125), channel_id=1, source_target_pairs={{0,2},{1,3},{2,0},{3,1},{4,6},{5,7},{6,4},{7,5},{8,10},{9,11},{10,... | collective-permute-start | bytes 221192 | tf_op jit(solution)/shard_map/ppermute | solution.py:245
  33.0 11.4 %collective-permute-start.24 = (bf16[48,768]{1,0:T(8,128)(2,1)S(1)}, bf16[48,768]{1,0:T(8,128)(2,1)S(1)}, u32[]{:S(2)}, u32[]{:S(2)}) collective-permute-start(bf16[48,768]{1,0:T(8,128)(2,1)S(1)} %get-tuple-element.125), channel_id=1, source_target_pairs={{0,4},{1,5},{2,6},{3,7},{4,0},{5,1},{6,2},{7,3},{8,12},{9,13},{10,... | collective-permute-start | bytes 221192 | tf_op jit(solution)/shard_map/ppermute | solution.py:245
  35.3 9.2 %collective-permute-start.23 = (bf16[48,768]{1,0:T(8,128)(2,1)S(1)}, bf16[48,768]{1,0:T(8,128)(2,1)S(1)}, u32[]{:S(2)}, u32[]{:S(2)}) collective-permute-start(bf16[48,768]{1,0:T(8,128)(2,1)S(1)} %copy-done.75), channel_id=1, source_target_pairs={{0,4},{1,5},{2,6},{3,7},{4,0},{5,1},{6,2},{7,3},{8,12},{9,13},{10,... | collective-permute-start | bytes 221192 | tf_op jit(solution)/shard_map/ppermute | solution.py:245
  37.0 15.0 %collective-permute-start.27 = (bf16[48,768]{1,0:T(8,128)(2,1)S(1)}, bf16[48,768]{1,0:T(8,128)(2,1)}, u32[]{:S(2)}, u32[]{:S(2)}) collective-permute-start(bf16[48,768]{1,0:T(8,128)(2,1)S(1)} %copy-done.75), channel_id=1, source_target_pairs={{0,1},{1,0},{2,3},{3,2},{4,5},{5,4},{6,7},{7,6},{8,9},{9,8},{10,11... | collective-permute-start | bytes 221192 | tf_op jit(solution)/shard_map/ppermute | solution.py:245
  41.9 10.6 %collective-permute-start.28 = (bf16[48,768]{1,0:T(8,128)(2,1)S(1)}, bf16[48,768]{1,0:T(8,128)(2,1)S(1)}, u32[]{:S(2)}, u32[]{:S(2)}) collective-permute-start(bf16[48,768]{1,0:T(8,128)(2,1)S(1)} %get-tuple-element.125), channel_id=1, source_target_pairs={{0,1},{1,0},{2,3},{3,2},{4,5},{5,4},{6,7},{7,6},{8,9},{9,8},{10,11... | collective-permute-start | bytes 221192 | tf_op jit(solution)/shard_map/ppermute | solution.py:245
  42.3 14.4 %collective-permute-start.14 = (bf16[144,768]{1,0:T(8,128)(2,1)S(1)}, bf16[144,768]{1,0:T(8,128)(2,1)S(1)}, u32[]{:S(2)}, u32[]{:S(2)}) collective-permute-start(bf16[144,768]{1,0:T(8,128)(2,1)S(1)} %pad_maximum_fusion.17), channel_id=1, source_target_pairs={{0,2},{1,3},{2,0},{3,1},{4,6},{5,7},{6,4},{7,5},{8,10},{9,11},{10,... | collective-permute-start | bytes 663560 | tf_op jit(solution)/shard_map/ppermute | solution.py:245
  55.1 12.9 %collective-permute-start.15 = (bf16[144,768]{1,0:T(8,128)(2,1)S(1)}, bf16[144,768]{1,0:T(8,128)(2,1)S(1)}, u32[]{:S(2)}, u32[]{:S(2)}) collective-permute-start(bf16[144,768]{1,0:T(8,128)(2,1)S(1)} %pad_maximum_fusion.17), channel_id=1, source_target_pairs={{0,4},{1,5},{2,6},{3,7},{4,0},{5,1},{6,2},{7,3},{8,12},{9,13},{10,... | collective-permute-start | bytes 663560 | tf_op jit(solution)/shard_map/ppermute | solution.py:245
  56.7 12.7 %collective-permute-start.17 = (bf16[144,768]{1,0:T(8,128)(2,1)S(1)}, bf16[144,768]{1,0:T(8,128)(2,1)S(1)}, u32[]{:S(2)}, u32[]{:S(2)}) collective-permute-start(bf16[144,768]{1,0:T(8,128)(2,1)S(1)} %pad_maximum_fusion.17), channel_id=1, source_target_pairs={{0,1},{1,0},{2,3},{3,2},{4,5},{5,4},{6,7},{7,6},{8,9},{9,8},{10,11... | collective-permute-start | bytes 663560 | tf_op jit(solution)/shard_map/ppermute | solution.py:245
  56.8 12.8 %collective-permute-start.3 = (bf16[144,768]{1,0:T(8,128)(2,1)}, bf16[144,768]{1,0:T(8,128)(2,1)S(1)}, u32[]{:S(2)}, u32[]{:S(2)}) collective-permute-start(bf16[144,768]{1,0:T(8,128)(2,1)} %pad_maximum_fusion.16), channel_id=1, source_target_pairs={{0,1},{1,0},{2,3},{3,2},{4,5},{5,4},{6,7},{7,6},{8,9},{9,8},{10,11... | collective-permute-start | bytes 663560 | tf_op jit(solution)/shard_map/ppermute | solution.py:245
  62.1 24.9 %collective-permute-start.35 = (bf16[96,3072]{1,0:T(8,128)(2,1)}, bf16[96,3072]{1,0:T(8,128)(2,1)}, u32[]{:S(2)}, u32[]{:S(2)}) collective-permute-start(bf16[96,3072]{1,0:T(8,128)(2,1)} %param.32), channel_id=1, source_target_pairs={{0,2},{1,3},{2,0},{3,1},{4,6},{5,7},{6,4},{7,5},{8,10},{9,11},{10,... | collective-permute-start | bytes 1769480 | tf_op jit(solution)/shard_map/ppermute | solution.py:245
  68.0 13.9 %collective-permute-start.2 = (bf16[144,768]{1,0:T(8,128)(2,1)S(1)}, bf16[144,768]{1,0:T(8,128)(2,1)S(1)}, u32[]{:S(2)}, u32[]{:S(2)}) collective-permute-start(bf16[144,768]{1,0:T(8,128)(2,1)S(1)} %collective-permute-done), channel_id=1, source_target_pairs={{0,2},{1,3},{2,0},{3,1},{4,6},{5,7},{6,4},{7,5},{8,10},{9,11},{10,... | collective-permute-start | bytes 663560 | tf_op jit(solution)/shard_map/ppermute | solution.py:245
  69.4 12.5 %collective-permute-start.18 = (bf16[144,768]{1,0:T(8,128)(2,1)S(1)}, bf16[144,768]{1,0:T(8,128)(2,1)S(1)}, u32[]{:S(2)}, u32[]{:S(2)}) collective-permute-start(bf16[144,768]{1,0:T(8,128)(2,1)S(1)} %collective-permute-done.14), channel_id=1, source_target_pairs={{0,1},{1,0},{2,3},{3,2},{4,5},{5,4},{6,7},{7,6},{8,9},{9,8},{10,11... | collective-permute-start | bytes 663560 | tf_op jit(solution)/shard_map/ppermute | solution.py:245
  69.5 13.0 %collective-permute-start.5 = (bf16[144,768]{1,0:T(8,128)(2,1)S(1)}, bf16[144,768]{1,0:T(8,128)(2,1)S(1)}, u32[]{:S(2)}, u32[]{:S(2)}) collective-permute-start(bf16[144,768]{1,0:T(8,128)(2,1)S(1)} %collective-permute-done.1), channel_id=1, source_target_pairs={{0,1},{1,0},{2,3},{3,2},{4,5},{5,4},{6,7},{7,6},{8,9},{9,8},{10,11... | collective-permute-start | bytes 663560 | tf_op jit(solution)/shard_map/ppermute | solution.py:245
  71.9 17.4 %collective-permute-start.36 = (bf16[96,3072]{1,0:T(8,128)(2,1)}, bf16[96,3072]{1,0:T(8,128)(2,1)}, u32[]{:S(2)}, u32[]{:S(2)}) collective-permute-start(bf16[96,3072]{1,0:T(8,128)(2,1)} %param.32), channel_id=1, source_target_pairs={{0,4},{1,5},{2,6},{3,7},{4,0},{5,1},{6,2},{7,3},{8,12},{9,13},{10,... | collective-permute-start | bytes 1769480 | tf_op jit(solution)/shard_map/ppermute | solution.py:245
  81.9 69.9 %collective-permute-start.38 = (bf16[96,3072]{1,0:T(8,128)(2,1)}, bf16[96,3072]{1,0:T(8,128)(2,1)}, u32[]{:S(2)}, u32[]{:S(2)}) collective-permute-start(bf16[96,3072]{1,0:T(8,128)(2,1)} %param.32), channel_id=1, source_target_pairs={{0,1},{1,0},{2,3},{3,2},{4,5},{5,4},{6,7},{7,6},{8,9},{9,8},{10,11... | collective-permute-start | bytes 1769480 | tf_op jit(solution)/shard_map/ppermute | solution.py:245
  81.9 17.8 %collective-permute-start.42 = (bf16[384,768]{1,0:T(8,128)(2,1)}, bf16[384,768]{1,0:T(8,128)(2,1)S(1)}, u32[]{:S(2)}, u32[]{:S(2)}) collective-permute-start(bf16[384,768]{1,0:T(8,128)(2,1)} %param.34), channel_id=1, source_target_pairs={{0,4},{1,5},{2,6},{3,7},{4,0},{5,1},{6,2},{7,3},{8,12},{9,13},{10,... | collective-permute-start | bytes 1769480 | tf_op jit(solution)/shard_map/ppermute | solution.py:245
  86.5 15.7 %collective-permute-start.43 = (bf16[384,768]{1,0:T(8,128)(2,1)}, bf16[384,768]{1,0:T(8,128)(2,1)S(1)}, u32[]{:S(2)}, u32[]{:S(2)}) collective-permute-start(bf16[384,768]{1,0:T(8,128)(2,1)} %param.34), channel_id=1, source_target_pairs={{0,2},{1,3},{2,0},{3,1},{4,6},{5,7},{6,4},{7,5},{8,10},{9,11},{10,... | collective-permute-start | bytes 1769480 | tf_op jit(solution)/shard_map/ppermute | solution.py:245
  87.0 18.1 %collective-permute-start.33 = (bf16[48,768]{1,0:T(8,128)(2,1)S(1)}, bf16[48,768]{1,0:T(8,128)(2,1)S(1)}, u32[]{:S(2)}, u32[]{:S(2)}) collective-permute-start(bf16[48,768]{1,0:T(8,128)(2,1)S(1)} %collective-permute-done.25), channel_id=1, source_target_pairs={{0,1},{1,0},{2,3},{3,2},{4,5},{5,4},{6,7},{7,6},{8,9},{9,8},{10,11... | collective-permute-start | bytes 221192 | tf_op jit(solution)/shard_map/ppermute | solution.py:245
  89.3 13.8 %collective-permute-start.20 = (bf16[144,768]{1,0:T(8,128)(2,1)S(1)}, bf16[144,768]{1,0:T(8,128)(2,1)S(1)}, u32[]{:S(2)}, u32[]{:S(2)}) collective-permute-start(bf16[144,768]{1,0:T(8,128)(2,1)S(1)} %collective-permute-done.16), channel_id=1, source_target_pairs={{0,1},{1,0},{2,3},{3,2},{4,5},{5,4},{6,7},{7,6},{8,9},{9,8},{10,11... | collective-permute-start | bytes 663560 | tf_op jit(solution)/shard_map/ppermute | solution.py:245
  103.1 62.3 %collective-permute-start.45 = (bf16[384,768]{1,0:T(8,128)(2,1)}, bf16[384,768]{1,0:T(8,128)(2,1)}, u32[]{:S(2)}, u32[]{:S(2)}) collective-permute-start(bf16[384,768]{1,0:T(8,128)(2,1)} %param.34), channel_id=1, source_target_pairs={{0,1},{1,0},{2,3},{3,2},{4,5},{5,4},{6,7},{7,6},{8,9},{9,8},{10,11... | collective-permute-start | bytes 1769480 | tf_op jit(solution)/shard_map/ppermute | solution.py:245
  103.6 45.1 %collective-permute-start.37 = (bf16[96,3072]{1,0:T(8,128)(2,1)}, bf16[96,3072]{1,0:T(8,128)(2,1)}, u32[]{:S(2)}, u32[]{:S(2)}) collective-permute-start(bf16[96,3072]{1,0:T(8,128)(2,1)} %collective-permute-done.35), channel_id=1, source_target_pairs={{0,4},{1,5},{2,6},{3,7},{4,0},{5,1},{6,2},{7,3},{8,12},{9,13},{10,... | collective-permute-start | bytes 1769480 | tf_op jit(solution)/shard_map/ppermute | solution.py:245
  105.1 62.7 %collective-permute-start.39 = (bf16[96,3072]{1,0:T(8,128)(2,1)}, bf16[96,3072]{1,0:T(8,128)(2,1)}, u32[]{:S(2)}, u32[]{:S(2)}) collective-permute-start(bf16[96,3072]{1,0:T(8,128)(2,1)} %collective-permute-done.35), channel_id=1, source_target_pairs={{0,1},{1,0},{2,3},{3,2},{4,5},{5,4},{6,7},{7,6},{8,9},{9,8},{10,11... | collective-permute-start | bytes 1769480 | tf_op jit(solution)/shard_map/ppermute | solution.py:245
  105.2 66.3 %collective-permute-start.40 = (bf16[96,3072]{1,0:T(8,128)(2,1)}, bf16[96,3072]{1,0:T(8,128)(2,1)}, u32[]{:S(2)}, u32[]{:S(2)}) collective-permute-start(bf16[96,3072]{1,0:T(8,128)(2,1)} %collective-permute-done.36), channel_id=1, source_target_pairs={{0,1},{1,0},{2,3},{3,2},{4,5},{5,4},{6,7},{7,6},{8,9},{9,8},{10,11... | collective-permute-start | bytes 1769480 | tf_op jit(solution)/shard_map/ppermute | solution.py:245
  149.2 15.3 %collective-permute-start.44 = (bf16[384,768]{1,0:T(8,128)(2,1)S(1)}, bf16[384,768]{1,0:T(8,128)(2,1)S(1)}, u32[]{:S(2)}, u32[]{:S(2)}) collective-permute-start(bf16[384,768]{1,0:T(8,128)(2,1)S(1)} %copy-done.68), channel_id=1, source_target_pairs={{0,2},{1,3},{2,0},{3,1},{4,6},{5,7},{6,4},{7,5},{8,10},{9,11},{10,... | collective-permute-start | bytes 1769480 | tf_op jit(solution)/shard_map/ppermute | solution.py:245
  151.8 18.0 %collective-permute-start.46 = (bf16[384,768]{1,0:T(8,128)(2,1)S(1)}, bf16[384,768]{1,0:T(8,128)(2,1)S(1)}, u32[]{:S(2)}, u32[]{:S(2)}) collective-permute-start(bf16[384,768]{1,0:T(8,128)(2,1)S(1)} %copy-done.68), channel_id=1, source_target_pairs={{0,1},{1,0},{2,3},{3,2},{4,5},{5,4},{6,7},{7,6},{8,9},{9,8},{10,11... | collective-permute-start | bytes 1769480 | tf_op jit(solution)/shard_map/ppermute | solution.py:245
  167.8 45.8 %collective-permute-start.48 = (bf16[384,768]{1,0:T(8,128)(2,1)S(1)}, bf16[384,768]{1,0:T(8,128)(2,1)S(1)}, u32[]{:S(2)}, u32[]{:S(2)}) collective-permute-start(bf16[384,768]{1,0:T(8,128)(2,1)S(1)} %collective-permute-done.44), channel_id=1, source_target_pairs={{0,1},{1,0},{2,3},{3,2},{4,5},{5,4},{6,7},{7,6},{8,9},{9,8},{10,11... | collective-permute-start | bytes 1769480 | tf_op jit(solution)/shard_map/ppermute | solution.py:245
  373.6 111.9 %collective-permute-start.91 = (bf16[1536,768]{1,0:T(8,128)(2,1)}, bf16[1536,768]{1,0:T(8,128)(2,1)}, u32[]{:S(2)}, u32[]{:S(2)}) collective-permute-start(bf16[1536,768]{1,0:T(8,128)(2,1)} %pad_maximum_fusion.2), channel_id=1, source_target_pairs={{0,1},{1,0},{2,3},{3,2},{4,5},{5,4},{6,7},{7,6},{8,9},{9,8},{10,11... | collective-permute-start | bytes 7077896 | tf_op jit(solution)/shard_map/ppermute | solution.py:245
  375.7 28.9 %collective-permute-start.56 = (bf16[64,96]{1,0:T(8,128)(2,1)S(1)}, bf16[64,96]{1,0:T(8,128)(2,1)S(1)}, u32[]{:S(2)}, u32[]{:S(2)}) collective-permute-start(bf16[64,96]{1,0:T(8,128)(2,1)S(1)} %pad_maximum_fusion.22), channel_id=1, source_target_pairs={{0,1},{1,0},{2,3},{3,2},{4,5},{5,4},{6,7},{7,6},{8,9},{9,8},{10,11... | collective-permute-start | bytes 36872 | tf_op jit(solution)/shard_map/ppermute | solution.py:245
  387.6 101.5 %collective-permute-start.84 = (bf16[384,3072]{1,0:T(8,128)(2,1)}, bf16[384,3072]{1,0:T(8,128)(2,1)}, u32[]{:S(2)}, u32[]{:S(2)}) collective-permute-start(bf16[384,3072]{1,0:T(8,128)(2,1)} %pad_maximum_fusion.1), channel_id=1, source_target_pairs={{0,1},{1,0},{2,3},{3,2},{4,5},{5,4},{6,7},{7,6},{8,9},{9,8},{10,11... | collective-permute-start | bytes 7077896 | tf_op jit(solution)/shard_map/ppermute | solution.py:245
  390.7 39.1 %collective-permute-start.77 = (bf16[384,768]{1,0:T(8,128)(2,1)}, bf16[384,768]{1,0:T(8,128)(2,1)}, u32[]{:S(2)}, u32[]{:S(2)}) collective-permute-start(bf16[384,768]{1,0:T(8,128)(2,1)} %pad_maximum_fusion.9), channel_id=1, source_target_pairs={{0,1},{1,0},{2,3},{3,2},{4,5},{5,4},{6,7},{7,6},{8,9},{9,8},{10,11... | collective-permute-start | bytes 1769480 | tf_op jit(solution)/shard_map/ppermute | solution.py:245
  394.1 37.3 %collective-permute-start.70 = (bf16[384,768]{1,0:T(8,128)(2,1)}, bf16[384,768]{1,0:T(8,128)(2,1)}, u32[]{:S(2)}, u32[]{:S(2)}) collective-permute-start(bf16[384,768]{1,0:T(8,128)(2,1)} %pad_maximum_fusion.8), channel_id=1, source_target_pairs={{0,1},{1,0},{2,3},{3,2},{4,5},{5,4},{6,7},{7,6},{8,9},{9,8},{10,11... | collective-permute-start | bytes 1769480 | tf_op jit(solution)/shard_map/ppermute | solution.py:245
  431.5 9.9 %collective-permute-start.78 = (bf16[192,768]{1,0:T(8,128)(2,1)S(1)}, bf16[192,768]{1,0:T(8,128)(2,1)S(1)}, u32[]{:S(2)}, u32[]{:S(2)}) collective-permute-start(bf16[192,768]{1,0:T(8,128)(2,1)S(1)} %pad_maximum_fusion.13), channel_id=1, source_target_pairs={{0,2},{1,3},{2,0},{3,1},{4,6},{5,7},{6,4},{7,5},{8,10},{9,11},{10,... | collective-permute-start | bytes 884744 | tf_op jit(solution)/shard_map/ppermute | solution.py:245
  433.2 14.5 %collective-permute-start.71 = (bf16[192,768]{1,0:T(8,128)(2,1)S(1)}, bf16[192,768]{1,0:T(8,128)(2,1)S(1)}, u32[]{:S(2)}, u32[]{:S(2)}) collective-permute-start(bf16[192,768]{1,0:T(8,128)(2,1)S(1)} %pad_maximum_fusion.12), channel_id=1, source_target_pairs={{0,2},{1,3},{2,0},{3,1},{4,6},{5,7},{6,4},{7,5},{8,10},{9,11},{10,... | collective-permute-start | bytes 884744 | tf_op jit(solution)/shard_map/ppermute | solution.py:245
  435.8 13.5 %collective-permute-start.64 = (bf16[192,768]{1,0:T(8,128)(2,1)S(1)}, bf16[192,768]{1,0:T(8,128)(2,1)S(1)}, u32[]{:S(2)}, u32[]{:S(2)}) collective-permute-start(bf16[192,768]{1,0:T(8,128)(2,1)S(1)} %pad_maximum_fusion.11), channel_id=1, source_target_pairs={{0,4},{1,5},{2,6},{3,7},{4,0},{5,1},{6,2},{7,3},{8,12},{9,13},{10,... | collective-permute-start | bytes 884744 | tf_op jit(solution)/shard_map/ppermute | solution.py:245
  441.4 11.7 %collective-permute-start.50 = (bf16[192,768]{1,0:T(8,128)(2,1)S(1)}, bf16[192,768]{1,0:T(8,128)(2,1)S(1)}, u32[]{:S(2)}, u32[]{:S(2)}) collective-permute-start(bf16[192,768]{1,0:T(8,128)(2,1)S(1)} %pad_maximum_fusion.10), channel_id=1, source_target_pairs={{0,2},{1,3},{2,0},{3,1},{4,6},{5,7},{6,4},{7,5},{8,10},{9,11},{10,... | collective-permute-start | bytes 884744 | tf_op jit(solution)/shard_map/ppermute | solution.py:245
  480.6 11.6 %collective-permute-start.76 = (bf16[48,768]{1,0:T(8,128)(2,1)S(1)}, bf16[48,768]{1,0:T(8,128)(2,1)S(1)}, u32[]{:S(2)}, u32[]{:S(2)}) collective-permute-start(bf16[48,768]{1,0:T(8,128)(2,1)S(1)} %pad_maximum_fusion.20), channel_id=1, source_target_pairs={{0,8},{8,0},{16,24},{24,16},{1,9},{9,1},{17,25},{25,17},{2,10},{10... | collective-permute-start | bytes 221192 | tf_op jit(solution)/shard_map/ppermute | solution.py:245
  482.4 10.5 %collective-permute-start.69 = (bf16[48,768]{1,0:T(8,128)(2,1)S(1)}, bf16[48,768]{1,0:T(8,128)(2,1)S(1)}, u32[]{:S(2)}, u32[]{:S(2)}) collective-permute-start(bf16[48,768]{1,0:T(8,128)(2,1)S(1)} %pad_maximum_fusion.19), channel_id=1, source_target_pairs={{0,8},{8,0},{16,24},{24,16},{1,9},{9,1},{17,25},{25,17},{2,10},{10... | collective-permute-start | bytes 221192 | tf_op jit(solution)/shard_map/ppermute | solution.py:245
  484.1 9.7 %collective-permute-start.55 = (bf16[48,768]{1,0:T(8,128)(2,1)S(1)}, bf16[48,768]{1,0:T(8,128)(2,1)S(1)}, u32[]{:S(2)}, u32[]{:S(2)}) collective-permute-start(bf16[48,768]{1,0:T(8,128)(2,1)S(1)} %pad_maximum_fusion.18), channel_id=1, source_target_pairs={{0,8},{8,0},{16,24},{24,16},{1,9},{9,1},{17,25},{25,17},{2,10},{10... | collective-permute-start | bytes 221192 | tf_op jit(solution)/shard_map/ppermute | solution.py:245
  487.5 22.0 %collective-permute-start.92 = (bf16[768,768]{1,0:T(8,128)(2,1)S(1)}, bf16[768,768]{1,0:T(8,128)(2,1)S(1)}, u32[]{:S(2)}, u32[]{:S(2)}) collective-permute-start(bf16[768,768]{1,0:T(8,128)(2,1)S(1)} %pad_maximum_fusion.5), channel_id=1, source_target_pairs={{0,4},{1,5},{2,6},{3,7},{4,0},{5,1},{6,2},{7,3},{8,12},{9,13},{10,... | collective-permute-start | bytes 3538952 | tf_op jit(solution)/shard_map/ppermute | solution.py:245
  490.8 27.9 %collective-permute-start.85 = (bf16[192,3072]{1,0:T(8,128)(2,1)S(1)}, bf16[192,3072]{1,0:T(8,128)(2,1)S(1)}, u32[]{:S(2)}, u32[]{:S(2)}) collective-permute-start(bf16[192,3072]{1,0:T(8,128)(2,1)S(1)} %pad_maximum_fusion.4), channel_id=1, source_target_pairs={{0,2},{1,3},{2,0},{3,1},{4,6},{5,7},{6,4},{7,5},{8,10},{9,11},{10,... | collective-permute-start | bytes 3538952 | tf_op jit(solution)/shard_map/ppermute | solution.py:245
  510.9 14.4 %collective-permute-start.93 = (bf16[384,768]{1,0:T(8,128)(2,1)S(1)}, bf16[384,768]{1,0:T(8,128)(2,1)S(1)}, u32[]{:S(2)}, u32[]{:S(2)}) collective-permute-start(bf16[384,768]{1,0:T(8,128)(2,1)S(1)} %add_convert_fusion.13), channel_id=1, source_target_pairs={{0,2},{1,3},{2,0},{3,1},{4,6},{5,7},{6,4},{7,5},{8,10},{9,11},{10,... | collective-permute-start | bytes 1769480 | tf_op jit(solution)/shard_map/ppermute | solution.py:245
  520.0 9.9 %collective-permute-start.86 = (bf16[96,3072]{1,0:T(8,128)(2,1)S(1)}, bf16[96,3072]{1,0:T(8,128)(2,1)S(1)}, u32[]{:S(2)}, u32[]{:S(2)}) collective-permute-start(bf16[96,3072]{1,0:T(8,128)(2,1)S(1)} %add_convert_fusion.20), channel_id=1, source_target_pairs={{0,4},{1,5},{2,6},{3,7},{4,0},{5,1},{6,2},{7,3},{8,12},{9,13},{10,... | collective-permute-start | bytes 1769480 | tf_op jit(solution)/shard_map/ppermute | solution.py:245
  527.0 9.9 %collective-permute-start.94 = (bf16[192,768]{1,0:T(8,128)(2,1)S(1)}, bf16[192,768]{1,0:T(8,128)(2,1)S(1)}, u32[]{:S(2)}, u32[]{:S(2)}) collective-permute-start(bf16[192,768]{1,0:T(8,128)(2,1)S(1)} %broadcast_select_fusion.2), channel_id=1, source_target_pairs={{0,8},{8,0},{16,24},{24,16},{1,9},{9,1},{17,25},{25,17},{2,10},{10... | collective-permute-start | bytes 884744 | tf_op jit(solution)/shard_map/ppermute | solution.py:245
  531.4 10.9 %collective-permute-start.87 = (bf16[48,3072]{1,0:T(8,128)(2,1)S(1)}, bf16[48,3072]{1,0:T(8,128)(2,1)S(1)}, u32[]{:S(2)}, u32[]{:S(2)}) collective-permute-start(bf16[48,3072]{1,0:T(8,128)(2,1)S(1)} %broadcast_select_fusion.5), channel_id=1, source_target_pairs={{0,8},{8,0},{16,24},{24,16},{1,9},{9,1},{17,25},{25,17},{2,10},{10... | collective-permute-start | bytes 884744 | tf_op jit(solution)/shard_map/ppermute | solution.py:245
  537.1 10.9 %collective-permute-start.95 = (bf16[96,768]{1,0:T(8,128)(2,1)S(1)}, bf16[96,768]{1,0:T(8,128)(2,1)S(1)}, u32[]{:S(2)}, u32[]{:S(2)}) collective-permute-start(bf16[96,768]{1,0:T(8,128)(2,1)S(1)} %broadcast_select_fusion.8), channel_id=1, source_target_pairs={{0,16},{8,24},{16,0},{24,8},{1,17},{9,25},{17,1},{25,9},{2,18},{10... | collective-permute-start | bytes 442376 | tf_op jit(solution)/shard_map/ppermute | solution.py:245
  (167 other events, 1748.9 us)

commit v2 on v1

v2 whole, which is shorter than its diff:
```python
import functools

import jax
import jax.numpy as jnp
from jax import lax
from jax.experimental import pallas as pl
from jax.experimental.pallas import tpu as pltpu
from jax.sharding import PartitionSpec as P

HEAD = 64
EPSILON = 1e-05
BLOCKED = -8000000000.0
LOW = jnp.bfloat16
F32 = jnp.float32
ANY = pl.BlockSpec(memory_space=pl.ANY)
NN = (((1,), (0,)), ((), ()))
NT = (((1,), (1,)), ((), ()))
TN = (((0,), (0,)), ((), ()))


def mm(a, b, dims=NN):
    return lax.dot_general(a, b, dims, preferred_element_type=F32)


def shape(dims, dtype=LOW):
    return jax.ShapeDtypeStruct(dims, dtype)


def whole(*dims):
    return pl.BlockSpec(dims, lambda *_: (0,) * len(dims))


def params(grid_rank):
    return pltpu.CompilerParams(
        dimension_semantics=("arbitrary",) * grid_rank, vmem_limit_bytes=60 * 2**20
    )


def cost(flops, nbytes, exps=0):
    return pl.CostEstimate(
        flops=int(flops), bytes_accessed=int(nbytes), transcendentals=int(exps)
    )


def bits_of(count):
    bits = [1 << i for i in range(count.bit_length() - 1)]
    assert count == 1 << len(bits), "axis size"
    return bits


def swap(x, bit, axis, count):
    return lax.ppermute(x, axis, [(i, i ^ bit) for i in range(count)])


def gather_rel(x, order, count):
    pieces = {0: x}
    for bit in order:
        pieces.update({m | bit: swap(p, bit, "fsdp", count) for m, p in list(pieces.items())})
    return [pieces[m] for m in range(count)]


def reorder(stacked, me):
    count = stacked.shape[0]
    bits = bits_of(count)
    x = stacked.reshape((2,) * len(bits) + stacked.shape[1:])
    for i, bit in enumerate(reversed(bits)):
        x = jnp.where((me & bit) != 0, jnp.flip(x, i), x)
    return x.reshape(stacked.shape)


def add_low(a, b):
    return (a.astype(F32) + b.astype(F32)).astype(LOW)


def reduce_chips(parts, order, count):
    for bit in order:
        sent = [m for m in sorted(parts) if m & bit]
        if len(sent) == 1:
            got = [swap(parts[sent[0]], bit, "fsdp", count)]
        else:
            got = swap(jnp.concatenate([parts[m] for m in sent], axis=0), bit, "fsdp", count)
            got = jnp.split(got, len(sent), axis=0)
        parts = {m ^ bit: add_low(parts[m ^ bit], g) for m, g in zip(sent, got)}
    return parts[0]


def sum_over_dp(x, count):
    at = lax.axis_index("dp")
    bits = bits_of(count)
    for bit in bits:
        low, high = jnp.split(x, 2, axis=0)
        upper = (at & bit) != 0
        got = swap(jnp.where(upper, low, high), bit, "dp", count)
        x = add_low(jnp.where(upper, high, low), got)
    for bit in reversed(bits):
        upper = (at & bit) != 0
        got = swap(x, bit, "dp", count)
        x = jnp.concatenate([jnp.where(upper, got, x), jnp.where(upper, x, got)], axis=0)
    return x


def place_rows(pieces, me):
    stacked = reorder(jnp.stack(pieces), me)
    return stacked.reshape((-1,) + pieces[0].shape[1:])


def copy_plan(sources, shard):
    plan = []
    for count, base, row, rows, target, offset in sources:
        for m in range(count):
            plan.append((base + m, row, rows, target, m, offset, shard))
    return plan


def run_copies(plan, me, operands, targets, sems):
    copies = []
    for i, (src, row, rows, target, m, offset, shard) in enumerate(plan):
        at = pl.multiple_of((me ^ m) * shard + offset, 16) if shard else offset
        copies.append(
            pltpu.make_async_copy(
                operands[src].at[pl.ds(row, rows), :],
                targets[target].at[pl.ds(at, rows), :],
                sems.at[i],
            )
        )
    for c in copies:
        c.start()
    return copies


def qkv_kernel(plan, count, info, tok, bias, *refs):
    pieces, (q, k, v, wq, wk, wv), sems = refs[:count], refs[count : count + 6], refs[count + 6]

    @pl.when(pl.program_id(0) == 0)
    def _():
        for c in run_copies(plan, info[0], pieces, (wq, wk, wv), sems):
            c.wait()

    rows = tok[...]
    q[...] = (mm(rows, wq[...]) + bias[0:1, :]).astype(LOW)
    k[...] = mm(rows, wk[...]).astype(LOW)
    v[...] = (mm(rows, wv[...]) + bias[1:2, :]).astype(LOW)


def qkv_call(info, tokens, bias, pieces, plan, tile=256):
    rows, model = tokens.shape
    row_block = pl.BlockSpec((tile, model), lambda i, _: (i, 0))
    return pl.pallas_call(
        functools.partial(qkv_kernel, plan, len(pieces)),
        out_shape=[shape((rows, model))] * 3 + [shape((model, model))] * 3,
        grid_spec=pltpu.PrefetchScalarGridSpec(
            num_scalar_prefetch=1,
            grid=(rows // tile,),
            in_specs=[row_block, whole(2, model)] + [ANY] * len(pieces),
            out_specs=[row_block] * 3 + [whole(model, model)] * 3,
            scratch_shapes=[pltpu.SemaphoreType.DMA((len(plan),))],
        ),
        compiler_params=params(1),
        cost_estimate=cost(6 * rows * model * model, 8 * rows * model + 12 * model * model),
        name="qkv",
    )(info, tokens, bias, *pieces)


def blocked_keys(info, micro, micros, slots):
    shift = slots.bit_length() - 3 + info[1 + micro]
    u = lax.broadcasted_iota(jnp.int32, (slots, 128), 0)
    j = lax.broadcasted_iota(jnp.int32, (slots, 128), 1) & (HEAD - 1)
    base = 1 + micros + 4 * micro
    limit = jnp.where(
        j < 2,
        jnp.where(j == 0, info[base], info[base + 1]),
        jnp.where(j == 2, info[base + 2], info[base + 3]),
    )
    inside = u - (j << shift)
    fine = ((u >> shift) == j) & (inside < limit)
    return jnp.where((j < 4) & jnp.logical_not(fine), BLOCKED, 0.0).astype(LOW)


def segment_rows(info, micro, slots):
    shift = slots.bit_length() - 3 + info[1 + micro]
    j = lax.broadcasted_iota(jnp.int32, (HEAD, slots), 0)
    t = lax.broadcasted_iota(jnp.int32, (HEAD, slots), 1)
    return jnp.where((t >> shift) == j, 1.0, 0.0).astype(LOW)


def attend_kernel(micros, info, q, k, v, context, probs, blocked, segments):
    micro = pl.program_id(0)
    slots = q.shape[0]

    @pl.when(pl.program_id(1) == 0)
    def _():
        blocked[...] = blocked_keys(info, micro, micros, slots)
        segments[...] = segment_rows(info, micro, slots)

    keys = k[...]
    q_t = q[...].T
    v_t = v[...].T
    lane = lax.broadcasted_iota(jnp.int32, keys.shape, 1)
    seg = segments[...]
    block = blocked[...]
    factor = 0.125 * 1.4426950408889634
    parts = []
    for h in range(2):
        mine = (lane < HEAD) if h == 0 else (lane >= HEAD)
        left = jnp.where(mine, keys, block)
        mine_q = q_t[h * HEAD : (h + 1) * HEAD]
        right = jnp.concatenate([mine_q, seg] if h == 0 else [seg, mine_q], axis=0)
        scores = mm(left, right)
        top = jnp.max(scores, axis=0, keepdims=True)
        exps = jnp.exp2(scores * factor - top * factor)
        total = jnp.sum(exps, axis=0, keepdims=True)
        low = (exps * (1.0 / total)).astype(LOW)
        probs[h] = low
        parts.append(mm(v_t[h * HEAD : (h + 1) * HEAD], low))
    context[...] = jnp.concatenate(parts, axis=0).T.astype(LOW)


def attend_call(info, q, k, v, micros):
    rows, model = q.shape
    slots, pairs = rows // micros, model // 128
    pair = pl.BlockSpec((slots, 128), lambda i, j, _: (i, j))
    return pl.pallas_call(
        functools.partial(attend_kernel, micros),
        out_shape=[shape((rows, model)), shape((micros * 2 * pairs, slots, slots))],
        grid_spec=pltpu.PrefetchScalarGridSpec(
            num_scalar_prefetch=1,
            grid=(micros, pairs),
            in_specs=[pair] * 3,
            out_specs=[
                pair,
                pl.BlockSpec((2, slots, slots), lambda i, j, _: (i * pairs + j, 0, 0)),
            ],
            scratch_shapes=[pltpu.VMEM((slots, 128), LOW), pltpu.VMEM((HEAD, slots), LOW)],
        ),
        compiler_params=params(2),
        cost_estimate=cost(
            16 * rows * slots * model,
            8 * rows * model + 4 * rows * slots * pairs,
            2 * rows * slots * pairs,
        ),
        name="attend",
    )(info, q, k, v)


def normal(x):
    mean = jnp.mean(x, axis=-1, keepdims=True)
    centered = x - mean
    variance = jnp.mean(centered * centered, axis=-1, keepdims=True)
    scale = lax.rsqrt(variance + EPSILON)
    return centered * scale, scale


def normal_back(e, n, scale):
    first = jnp.mean(e, axis=-1, keepdims=True)
    second = jnp.mean(e * n, axis=-1, keepdims=True)
    return (e - first - n * second) * scale


def gelu_both(x):
    size = jnp.abs(x)
    t = 1.0 / (1.0 + size * (0.3275911 * 0.7071067811865476))
    e = jnp.exp2(x * x * (-0.5 * 1.4426950408889634))
    series = 0.5 * 1.061405429
    for c in (-1.453152027, 1.421413741, -0.284496736, 0.254829592):
        series = series * t + 0.5 * c
    tail = series * t * e
    phi = jnp.where(x >= 0, 1.0 - tail, tail)
    return x * phi, phi + x * e * 0.3989422804014327


def colsum(x):
    return jnp.sum(x, axis=0, keepdims=True)


def middle_kernel(
    plan, count, micros, slots, info, tok, ctx, cot, vec, b_up, *refs
):
    pieces = refs[:count]
    (out, active, d_up, hid_low, d_down, d_res, d_att, d_ctx, sums, sum_up) = refs[
        count : count + 10
    ]
    wo, wu, wd, slope, sems = refs[count + 10 :]
    step = pl.program_id(0)

    @pl.when(step == 0)
    def _():
        for c in run_copies(plan, info[0], pieces, (wo, wu, wd), sems):
            c.wait()
        sums[...] = jnp.zeros_like(sums)
        sum_up[...] = jnp.zeros_like(sum_up)

    tile, model = tok.shape
    inner = active.shape[1]
    part = 768
    b_out, gain_1, shift_1 = vec[0:1, :], vec[1:2, :], vec[2:3, :]
    b_down, gain_2, shift_2 = vec[3:4, :], vec[4:5, :], vec[5:6, :]
    res_1 = tok[...].astype(F32) + (mm(ctx[...], wo[...]) + b_out)
    n_1, s_1 = normal(res_1)
    hidden = n_1 * gain_1 + shift_1
    low = hidden.astype(LOW)
    hid_low[...] = low
    down = jnp.zeros((tile, model), F32)
    for c in range(0, inner, part):
        x = mm(low, wu[:, c : c + part]) + b_up[:, c : c + part]
        a, g = gelu_both(x)
        a = a.astype(LOW)
        active[:, c : c + part] = a
        slope[:, c : c + part] = g
        down = down + mm(a, wd[c : c + part, :])
    n_2, s_2 = normal(hidden + (down + b_down))
    out[...] = (n_2 * gain_2 + shift_2).astype(LOW)

    per_micro = slots // tile
    micro = step // per_micro
    shift = slots.bit_length() - 3 + info[1 + micro]
    t = lax.broadcasted_iota(jnp.int32, (tile, 1), 0) + (step - micro * per_micro) * tile
    seg = t >> shift
    base = 1 + micros + 4 * micro
    limit = jnp.where(
        seg < 2,
        jnp.where(seg == 0, info[base], info[base + 1]),
        jnp.where(seg == 2, info[base + 2], info[base + 3]),
    )
    live = (t - (seg << shift)) < limit
    grad = jnp.where(live, cot[...].astype(F32), 0.0)
    d_2 = normal_back(grad * gain_2, n_2, s_2)
    dd = d_2.astype(LOW)
    d_down[...] = dd
    sums[0:1, :] += colsum(grad * n_2)
    sums[1:2, :] += colsum(grad)
    sums[2:3, :] += colsum(dd.astype(F32))
    d_hid = d_2
    for c in range(0, inner, part):
        g = mm(dd, wd[c : c + part, :], NT) * slope[:, c : c + part]
        g = g.astype(LOW)
        d_up[:, c : c + part] = g
        sum_up[:, c : c + part] += colsum(g.astype(F32))
        d_hid = d_hid + mm(g, wu[:, c : c + part], NT)
    d_1 = normal_back(d_hid * gain_1, n_1, s_1)
    d_res[...] = d_1
    da = d_1.astype(LOW)
    d_att[...] = da
    sums[3:4, :] += colsum(d_hid * n_1)
    sums[4:5, :] += colsum(d_hid)
    sums[5:6, :] += colsum(da.astype(F32))
    d_ctx[...] = mm(da, wo[...], NT).astype(LOW)


def middle_call(info, tokens, context, cotangent, vec, b_up, pieces, plan, micros, tile=256):
    rows, model = tokens.shape
    inner = b_up.shape[1]
    row = pl.BlockSpec((tile, model), lambda i, _: (i, 0))
    wide = pl.BlockSpec((tile, inner), lambda i, _: (i, 0))
    return pl.pallas_call(
        functools.partial(middle_kernel, plan, len(pieces), micros, rows // micros),
        out_shape=[
            shape((rows, model)),
            shape((rows, inner)),
            shape((rows, inner)),
            shape((rows, model)),
            shape((rows, model)),
            shape((rows, model), F32),
            shape((rows, model)),
            shape((rows, model)),
            shape((8, model), F32),
            shape((1, inner), F32),
        ],
        grid_spec=pltpu.PrefetchScalarGridSpec(
            num_scalar_prefetch=1,
            grid=(rows // tile,),
            in_specs=[row] * 3 + [whole(*vec.shape), whole(1, inner)] + [ANY] * len(pieces),
            out_specs=[row, wide, wide, row, row, row, row, row, whole(8, model), whole(1, inner)],
            scratch_shapes=[
                pltpu.VMEM((model, model), LOW),
                pltpu.VMEM((model, inner), LOW),
                pltpu.VMEM((inner, model), LOW),
                pltpu.VMEM((tile, inner), F32),
                pltpu.SemaphoreType.DMA((len(plan),)),
            ],
        ),
        compiler_params=params(1),
        cost_estimate=cost(
            8 * rows * model * inner + 4 * rows * model * model,
            20 * rows * model + 4 * rows * inner + 4 * model * inner,
            2 * rows * inner,
        ),
        name="middle",
    )(info, tokens, context, cotangent, vec, b_up, *pieces)


def attend_back_kernel(q, k, v, ctx, d_ctx, probs, grads, sums):
    keys, queries, values, d_c = k[...], q[...], v[...], d_ctx[...]
    k_t = keys.T
    d_t = d_c.T
    c_t = ctx[...].T
    lane = lax.broadcasted_iota(jnp.int32, keys.shape, 1)
    row = lax.broadcasted_iota(jnp.int32, d_t.shape, 0)
    spread = d_t.astype(F32) * c_t.astype(F32)
    d_q, d_k, d_v = [], [], []
    for h in range(2):
        part = slice(h * HEAD, (h + 1) * HEAD)
        delta = colsum(spread[part])
        mine = (row < HEAD) if h == 0 else (row >= HEAD)
        d_p = mm(values, jnp.where(mine, d_t, jnp.zeros_like(d_t)))
        p = probs[h]
        d_s = (p.astype(F32) * (d_p - delta)).astype(LOW)
        d_v.append(mm(p, d_c))
        d_k.append(mm(d_s, queries))
        d_q.append(mm(k_t[part], d_s))
    left = lane < HEAD
    dq = (jnp.concatenate(d_q, axis=0).T * 0.125).astype(LOW)
    dk = (jnp.where(left, d_k[0], d_k[1]) * 0.125).astype(LOW)
    dv = jnp.where(left, d_v[0], d_v[1]).astype(LOW)
    grads[0], grads[1], grads[2] = dq, dk, dv
    sums[0, 0:1, :] = colsum(dq.astype(F32))
    sums[0, 1:2, :] = colsum(dv.astype(F32))


def attend_back_call(q, k, v, context, d_context, probs, micros):
    rows, model = q.shape
    slots, pairs = rows // micros, model // 128
    pair = pl.BlockSpec((slots, 128), lambda i, j: (i, j))
    return pl.pallas_call(
        attend_back_kernel,
        out_shape=[shape((3, rows, model)), shape((micros, 8, model), F32)],
        grid=(micros, pairs),
        in_specs=[pair] * 5
        + [pl.BlockSpec((2, slots, slots), lambda i, j: (i * pairs + j, 0, 0))],
        out_specs=[
            pl.BlockSpec((3, slots, 128), lambda i, j: (0, i, j)),
            pl.BlockSpec((1, 8, 128), lambda i, j: (i, 0, j)),
        ],
        compiler_params=params(2),
        cost_estimate=cost(
            32 * rows * slots * model, 16 * rows * model + 4 * rows * slots * pairs
        ),
        name="attend_back",
    )(q, k, v, context, d_context, probs)


def wide_rows_kernel(info, left, right, *refs):
    acc = mm(left[...], right[...], TN)
    if len(refs) == 2:
        acc = acc + refs[0][0].astype(F32)
    refs[-1][0] = acc.astype(LOW)


def wide_rows_call(info, left, right, fsdp, core, got=None):
    rows, inner = left.shape
    model = right.shape[1]
    shard, chips = inner // fsdp, fsdp // 2
    block = pl.BlockSpec((1, shard, model), lambda j, _: (j, 0, 0))
    extra = [] if got is None else [got]
    return pl.pallas_call(
        wide_rows_kernel,
        out_shape=shape((chips, shard, model)),
        grid_spec=pltpu.PrefetchScalarGridSpec(
            num_scalar_prefetch=1,
            grid=(chips,),
            in_specs=[
                pl.BlockSpec((rows, shard), lambda j, info: (0, info[0] ^ (2 * j + core))),
                whole(rows, model),
            ]
            + [block] * len(extra),
            out_specs=block,
        ),
        compiler_params=params(1),
        cost_estimate=cost(rows * inner * model, rows * inner + 2 * rows * model + inner * model),
        name="grad_rows",
    )(info, left, right, *extra)


def shards_kernel(fsdp, info, left, right, away, home, acc):
    me = info[0]
    right = right[0] if len(right.shape) == 3 else right[...]
    acc[...] = mm(left[...], right, TN)
    shard = acc.shape[0] // fsdp
    for m in range(fsdp):
        at = pl.multiple_of((me ^ m) * shard, 16)
        target = away if m & 1 else home
        target[m >> 1] = acc[pl.ds(at, shard), :].astype(LOW)


def shards_call(info, left, right, fsdp, block=768):
    rows, model = left.shape
    shard, chips = model // fsdp, fsdp // 2
    if right.ndim == 3:
        n, stacked = right.shape[2], right.shape[0]
        grid = (stacked,)
        spec = pl.BlockSpec((1, rows, n), lambda i, _: (i, 0, 0))
        out = shape((chips, stacked * shard, n))
        out_spec = pl.BlockSpec((chips, shard, n), lambda i, _: (0, i, 0))
        block = n
    else:
        n, stacked = right.shape[1], 1
        grid = (n // block,)
        spec = pl.BlockSpec((rows, block), lambda i, _: (0, i))
        out = shape((chips, shard, n))
        out_spec = pl.BlockSpec((chips, shard, block), lambda i, _: (0, 0, i))
    return pl.pallas_call(
        functools.partial(shards_kernel, fsdp),
        out_shape=[out, out],
        grid_spec=pltpu.PrefetchScalarGridSpec(
            num_scalar_prefetch=1,
            grid=grid,
            in_specs=[whole(rows, model), spec],
            out_specs=[out_spec, out_spec],
            scratch_shapes=[pltpu.VMEM((model, block), F32)],
        ),
        compiler_params=params(1),
        cost_estimate=cost(
            2 * rows * model * n * stacked,
            2 * rows * model + 2 * rows * n * stacked + 2 * model * n * stacked,
        ),
        name="grad_shards",
    )(info, left, right)


def token_kernel(d_res, grads, wq, wk, wv, out):
    out[...] = (
        d_res[...]
        + mm(grads[0], wq[...], NT)
        + mm(grads[1], wk[...], NT)
        + mm(grads[2], wv[...], NT)
    )


def token_call(d_res, grads, wq, wk, wv, tile=256):
    rows, model = d_res.shape
    row = pl.BlockSpec((tile, model), lambda i: (i, 0))
    return pl.pallas_call(
        token_kernel,
        out_shape=shape((rows, model), F32),
        grid=(rows // tile,),
        in_specs=[row, pl.BlockSpec((3, tile, model), lambda i: (0, i, 0))]
        + [whole(model, model)] * 3,
        out_specs=row,
        compiler_params=params(1),
        cost_estimate=cost(6 * rows * model * model, 14 * rows * model + 6 * model * model),
        name="grad_tokens",
    )(d_res, grads, wq, wk, wv)


VECTORS = (1, 4, 6, 7, 8, 12, 13, 14, 10)


def on_device(sizes, tokens, cotangent, bucket, lengths, *shards):
    dp, fsdp = sizes
    me = lax.axis_index("fsdp").astype(jnp.int32)
    chip_bits = bits_of(fsdp)[1:]
    up, down = chip_bits + [1], chip_bits[::-1] + [1]
    rows, model = tokens.shape
    inner = shards[9].shape[1]
    shard, inner_shard = shards[0].shape[0], shards[11].shape[0]
    micros = bucket.shape[0]
    half = shard // 2
    aligned = shard % 32 == 0 and inner_shard % 128 == 0
    info = jnp.concatenate([me[None], bucket, lengths.reshape(-1)])

    vecs = jnp.concatenate([shards[i].reshape(-1, shard) for i in VECTORS], axis=0)
    first = jnp.concatenate([shards[0], shards[2][:half]], axis=0)
    second = jnp.concatenate([shards[3], shards[2][half:]], axis=0)
    got_v = gather_rel(vecs, down, fsdp)
    got_1, got_2 = gather_rel(first, up, fsdp), gather_rel(second, down, fsdp)
    got_o = gather_rel(shards[5], up, fsdp)
    got_up, got_down = gather_rel(shards[9], up, fsdp), gather_rel(shards[11], down, fsdp)
    n_vec = vecs.shape[0]
    all_vecs = reorder(jnp.stack(got_v), me).astype(F32)
    narrow = all_vecs[:, :8].transpose(1, 0, 2).reshape(8, model)
    b_up = all_vecs[:, 8:].reshape(1, inner)

    if aligned:
        n = fsdp
        qkv_pieces = got_1 + got_2
        qkv_plan = copy_plan(
            [
                (n, 0, 0, shard, 0, 0),
                (n, 0, shard, half, 1, 0),
                (n, n, shard, shard - half, 1, half),
                (n, n, 0, shard, 2, 0),
            ],
            shard,
        )
        mid_pieces = got_o + got_up + got_down
        mid_plan = copy_plan([(n, 0, 0, shard, 0, 0), (n, n, 0, shard, 1, 0)], shard)
        mid_plan += copy_plan([(n, 2 * n, 0, inner_shard, 2, 0)], inner_shard)
    else:
        w_k = [jnp.concatenate([a[shard:], b[shard:]], axis=0) for a, b in zip(got_1, got_2)]
        qkv_pieces = [
            place_rows([p[:shard] for p in got_1], me),
            place_rows(w_k, me),
            place_rows([p[:shard] for p in got_2], me),
        ]
        qkv_plan = [(i, 0, model, i, 0, 0, 0) for i in range(3)]
        mid_pieces = [place_rows(p, me) for p in (got_o, got_up, got_down)]
        mid_plan = [(i, 0, (model, model, inner)[i], i, 0, 0, 0) for i in range(3)]

    q, k, v, wq, wk, wv = qkv_call(info, tokens, narrow[:2], qkv_pieces, qkv_plan)
    context, probs = attend_call(info, q, k, v, micros)
    (output, active, d_up, hid_low, d_down, d_res, d_att, d_ctx, sums, sum_up) = middle_call(
        info, tokens, context, cotangent, narrow[2:], b_up, mid_pieces, mid_plan, micros
    )

    rs_up, rs_down = chip_bits, chip_bits[::-1]

    def finish(parts, order):
        mine = reduce_chips({2 * j: parts[j] for j in range(fsdp // 2)}, order, fsdp)
        return sum_over_dp(mine, dp).astype(F32)

    def both_cores(away, home, order):
        got = swap(away, 1, "fsdp", fsdp)
        return finish([add_low(home[j], got[j]) for j in range(fsdp // 2)], order)

    def relative(full):
        n = full.shape[0] // fsdp
        r = reorder(full.astype(LOW).reshape(fsdp, n, full.shape[1]), me)
        r = r.reshape(fsdp // 2, 2, n, full.shape[1])
        return r[:, 1], r[:, 0]

    finals = [None] * 15
    if aligned:
        away = wide_rows_call(info, active, d_down, fsdp, 1)
        got = swap(away, 1, "fsdp", fsdp)
        home = wide_rows_call(info, active, d_down, fsdp, 0, got)
        finals[11] = finish([home[j] for j in range(fsdp // 2)], rs_down)
        finals[9] = both_cores(*shards_call(info, hid_low, d_up, fsdp), rs_up)
        finals[5] = both_cores(*shards_call(info, context, d_att, fsdp), rs_up)
    else:
        finals[11] = both_cores(*relative(mm(active, d_down, TN)), rs_down)
        finals[9] = both_cores(*relative(mm(hid_low, d_up, TN)), rs_up)
        finals[5] = both_cores(*relative(mm(context, d_att, TN)), rs_up)
    grads, qv_sums = attend_back_call(q, k, v, context, d_ctx, probs, micros)
    if aligned:
        three = both_cores(*shards_call(info, tokens, grads, fsdp), rs_down)
    else:
        parts = [relative(mm(tokens, grads[i], TN)) for i in range(3)]
        away, home = (jnp.concatenate([p[i] for p in parts], axis=1) for i in range(2))
        three = both_cores(away, home, rs_down)
    finals[0], finals[2], finals[3] = three[:shard], three[shard : 2 * shard], three[2 * shard :]
    token_grads = token_call(d_res, grads, wq, wk, wv)

    qv = jnp.sum(qv_sums, axis=0)
    narrow_sums = jnp.stack(
        [qv[0], qv[1], sums[5], sums[3], sums[4], sums[2], sums[0], sums[1]]
    )
    by_shard = jnp.concatenate(
        [narrow_sums.reshape(8, fsdp, shard).transpose(1, 0, 2), sum_up.reshape(fsdp, -1, shard)],
        axis=1,
    )
    pad = (-n_vec) % (2 * dp)
    by_shard = jnp.pad(by_shard, ((0, 0), (0, pad), (0, 0)))
    small = both_cores(*relative(by_shard.reshape(fsdp * (n_vec + pad), shard)), rs_up)
    at = 0
    for i in VECTORS:
        n = shards[i].shape[0] // shard
        finals[i] = small[at : at + n].reshape(-1)
        at += n
    return (output, token_grads) + tuple(finals)


def solution(mesh):
    placed = (
        P(("dp", "fsdp"), None),
        P(("dp", "fsdp"), None),
        P(("dp", "fsdp")),
        P(("dp", "fsdp"), None),
        P("fsdp", None),
        P("fsdp"),
        P("fsdp", None),
        P("fsdp", None),
        P("fsdp"),
        P("fsdp", None),
        P("fsdp"),
        P("fsdp"),
        P("fsdp"),
        P("fsdp", None),
        P("fsdp"),
        P("fsdp", None),
        P("fsdp"),
        P("fsdp"),
        P("fsdp"),
    )
    sizes = (mesh.shape["dp"], mesh.shape["fsdp"])
    return jax.shard_map(
        functools.partial(on_device, sizes),
        mesh=mesh,
        in_specs=placed,
        out_specs=(
            P(("dp", "fsdp"), None),
            P(("dp", "fsdp"), None),
            P("fsdp", None),
            P("fsdp"),
            P("fsdp", None),
            P("fsdp", None),
            P("fsdp"),
            P("fsdp", None),
            P("fsdp"),
            P("fsdp"),
            P("fsdp"),
            P("fsdp", None),
            P("fsdp"),
            P("fsdp", None),
            P("fsdp"),
            P("fsdp"),
            P("fsdp"),
        ),
        check_vma=False,
    )
```

time: 576 us -> 374 us (0.65); the launches traced: 568 us -> 372 us
  matrix products: 212 us -> 0 us
  Pallas kernels: 0 us -> 142 us
  other arithmetic: 77.1 us -> 15.2 us
  local copies, waits for them, and re-layouts: 69 us -> 10.3 us
  starting transfers between devices: 76.4 us -> 58.4 us
  waiting for transfers between devices: 128 us -> 145 us
    dot_general x48 -> x0, matrix products: 212 us -> none  [the longest x10 63.6 us: project(): jnp.dot(inputs_low, matrix, preferred_element_type=jnp.float32)]
    pallas_call x0 -> x10, Pallas kernels: none -> 142 us  [the longest x1 43.6 us: middle_call(): pl.pallas_call(functools.partial(middle_kernel, plan, len(pieces), micros...]
    convert_element_type x48 -> x30, other arithmetic: 41.1 us -> 9.48 us  [the longest x24 6.46 us: add_low(): return (a.astype(F32) + b.astype(F32)).astype(LOW)]
    dynamic_update_slice x42 -> x0, local copies, waits for them, and re-layouts: 31.5 us -> none  [place(): lax.dynamic_update_slice_in_dim(whole, piece, (me ^ m) * rows, axis=0)]
    ppermute x98 -> x77, starting transfers between devices: 76.4 us -> 58.4 us  [swap(): return lax.ppermute(x, axis, [(i, i ^ bit) for i in range(count)])]
    ppermute x98 -> x77, waiting for transfers between devices: 128 us -> 145 us  [swap(): return lax.ppermute(x, axis, [(i, i ^ bit) for i in range(count)])]
    unnamed x234 -> x79, local copies, waits for them, and re-layouts: 16.9 us -> 1.51 us
    reduce_sum x14 -> x1, other arithmetic: 14.5 us -> 0.8 us  [on_device(): qv = jnp.sum(qv_sums, axis=0)]
  transfers between devices with their start and end apart: 98 -> 77, of which waited for: 40 -> 30; matrix products, arithmetic and copies ran while one was open for 33% -> 5% of each run, Pallas kernels for 0% -> 21%
where the time goes in v2:
time: 374 us; the launch traced here: 372 us
  waiting for transfers between devices  145 us (39%)
  Pallas kernels  142 us (38%)
  starting transfers between devices  58.4 us (16%)
  other arithmetic  15.2 us (4%)
  local copies, waits for them, and re-layouts  10.3 us (3%)
    ppermute x77, waiting for transfers between devices, swap(): return lax.ppermute(x, axis, [(i, i ^ bit) for i in range(count)])  145 us
    ppermute x77, starting transfers between devices, swap(): return lax.ppermute(x, axis, [(i, i ^ bit) for i in range(count)])  58.4 us
    pallas_call x1, Pallas kernels, middle_call(): pl.pallas_call(functools.partial(middle_kernel, plan, len(pieces), micros...  43.6 us
    pallas_call x3, Pallas kernels, shards_call(): pl.pallas_call(functools.partial(shards_kernel, fsdp), out_shape=[out, ou...  23.7 us
    pallas_call x1, Pallas kernels, attend_call(): pl.pallas_call(functools.partial(attend_kernel, micros), out_shape=[shape...  21.5 us
    pallas_call x1, Pallas kernels, attend_back_call(): pl.pallas_call(attend_back_kernel, out_shape=[shape((3, rows, model)), sh...  19.8 us
    pallas_call x2, Pallas kernels, wide_rows_call(): pl.pallas_call(wide_rows_kernel, out_shape=shape((chips, shard, model)),...  14.6 us
    pallas_call x1, Pallas kernels, qkv_call(): pl.pallas_call(functools.partial(qkv_kernel, plan, len(pieces)), out_shap...  10 us
  transfers between devices with their start and end apart: 77, of which 30 were waited for; matrix products, arithmetic and copies ran while one was open for 5% of the time, Pallas kernels for 21%

profile of v2, /device:TPU:0, one launch (start us, length us, event | category | flops | bytes accessed | tf_op | source)
XLA Modules:
  0.0 372.4 jit_solution(11164257732451002952)
XLA Ops:
  2.9 2.6 collective-permute-start.1
  12.4 1.9 collective-permute-start.5
  16.1 2.0 collective-permute-start.8
  21.2 3.2 collective-permute-done.8.refs_2_
  24.4 5.9 %collective-permute-done.17.refs_12_ = bf16[144,768]{1,0:T(8,128)(2,1)S(1)} collective-permute-done((bf16[144,768]{1,0:T(8,128)(2,1)S(1)}, bf16[144,768]{1,0:T(8,128)(2,1)S(1)}, u32[]{:S(2)}, u32[]{:S(2)}) %collective-permute-start.17) | collective-permute-done | bytes 221216 | tf_op jit(solution)/shard_map/ppermute | solution.py:52
  34.0 1.9 collective-permute-done.26.refs_6_
  37.5 2.7 collective-permute-done.12.refs_6_
  40.3 12.5 %collective-permute-done.19.refs_14_ = bf16[144,768]{1,0:T(8,128)(2,1)S(1)} collective-permute-done((bf16[144,768]{1,0:T(8,128)(2,1)S(1)}, bf16[144,768]{1,0:T(8,128)(2,1)S(1)}, u32[]{:S(2)}, u32[]{:S(2)}) %collective-permute-start.19) | collective-permute-done | bytes 221216 | tf_op jit(solution)/shard_map/ppermute | solution.py:52
  59.5 20.1 %collective-permute-done.38.refs_20_ = bf16[384,768]{1,0:T(8,128)(2,1)S(1)} collective-permute-done((bf16[384,768]{1,0:T(8,128)(2,1)S(1)}, bf16[384,768]{1,0:T(8,128)(2,1)S(1)}, u32[]{:S(2)}, u32[]{:S(2)}) %collective-permute-start.38) | collective-permute-done | bytes 589856 | tf_op jit(solution)/shard_map/ppermute | solution.py:52
  85.0 10.0 %qkv.1 = (bf16[1024,768]{1,0:T(8,128)(2,1)}, bf16[1024,768]{1,0:T(8,128)(2,1)}, bf16[1024,768]{1,0:T(8,128)(2,1)}, bf16[768,768]{1,0:T(8,128)(2,1)}, bf16[768,768]{1,0:T(8,128)(2,1)}, /*index=5*/bf16[768,768]{1,0:T(8,128)(2,1)}) custom-call(s32[11]{0:T(128)} %pad_add_fusion.info, bf16[1024,768]{1,0:T(8,128)(2,1)} %left.1, f32[2,768]{1,0:T(2,128)} %slice.208.bias, ...), custom_call_target="tpu_custom_call" | custom-call | flops 3623878656 | bytes 13369344 | tf_op jit(solution)/shard_map/qkv/pallas_call | solution.py:148
  95.9 1.7 collective-permute-done.40.refs_22_
  98.1 21.5 %attend.1 = (bf16[1024,768]{1,0:T(8,128)(2,1)}, bf16[24,512,512]{2,1,0:T(8,128)(2,1)}) custom-call(s32[11]{0:T(128)} %pad_add_fusion.info, bf16[1024,768]{1,0:T(8,128)(2,1)} %get-tuple-element.43.q, bf16[1024,768]{1,0:T(8,128)(2,1)} %get-tuple-element.44.k, bf16[1024,768]{1,0:T(8,128)(2,1)} %get-tuple-element.45.v), custom_call_target="tpu_custom_call" | custom-call | flops 6442450944 | bytes 18874368 | tf_op jit(solution)/shard_map/attend/pallas_call | solution.py:222
  121.0 43.6 %middle.1 = (bf16[1024,768]{1,0:T(8,128)(2,1)}, bf16[1024,3072]{1,0:T(8,128)(2,1)}, bf16[1024,3072]{1,0:T(8,128)(2,1)}, bf16[1024,768]{1,0:T(8,128)(2,1)}, bf16[...) custom-call(s32[11]{0:T(128)} %pad_add_fusion.info, ...), custom_call_target="tpu_custom_call" | custom-call | flops 21743271936 | bytes 37748736 | tf_op jit(solution)/shard_map/middle/pallas_call | solution.py:354
  165.4 19.8 %attend_back.1 = (bf16[3,1024,768]{2,1,0:T(8,128)(2,1)}, f32[2,8,768]{2,1,0:T(8,128)}) custom-call(bf16[1024,768]{1,0:T(8,128)(2,1)} %get-tuple-element.43.q, bf16[1024,768]{1,0:T(8,128)(2,1)} %get-tuple-element.44.k, bf16[1024,768]{1,0:T(8,128)(2,1)} %get-tuple-element.45.v, bf16[1024,768]{1,0:T(8,128)(2,1)} %get-tuple-element.46.ctx.left, ...), custom_call_target="tpu_custom_call" | custom-call | flops 12884901888 | bytes 25165824 | tf_op jit(solution)/shard_map/attend_back/pallas_call | solution.py:423
  186.4 7.1 %grad_rows.2 = bf16[4,384,768]{2,1,0:T(8,128)(2,1)} custom-call(s32[11]{0:T(128)} %pad_add_fusion.info, bf16[1024,3072]{1,0:T(8,128)(2,1)} %get-tuple-element.67.left, bf16[1024,768]{1,0:T(8,128)(2,1)} %get-tuple-element.68.right), custom_call_target="tpu_custom_call" | custom-call | flops 2415919104 | bytes 7077888 | tf_op jit(solution)/shard_map/grad_rows/pallas_call | solution.py:454
  195.1 10.1 %grad_shards.5 = (bf16[4,96,3072]{2,1,0:T(8,128)(2,1)}, bf16[4,96,3072]{2,1,0:T(8,128)(2,1)}) custom-call(s32[11]{0:T(128)} %pad_add_fusion.info, bf16[1024,768]{1,0:T(8,128)(2,1)} %get-tuple-element.63.left, bf16[1024,3072]{1,0:T(8,128)(2,1)} %get-tuple-element.64.right), custom_call_target="tpu_custom_call" | custom-call | flops 4831838208 | bytes 12582912 | tf_op jit(solution)/shard_map/grad_shards/pallas_call | solution.py:500
  205.8 5.0 %grad_shards.4 = (bf16[4,96,768]{2,1,0:T(8,128)(2,1)}, bf16[4,96,768]{2,1,0:T(8,128)(2,1)}) custom-call(s32[11]{0:T(128)} %pad_add_fusion.info, bf16[1024,768]{1,0:T(8,128)(2,1)} %get-tuple-element.46.ctx.left, bf16[1024,768]{1,0:T(8,128)(2,1)} %get-tuple-element.60.right), custom_call_target="tpu_custom_call" | custom-call | flops 1207959552 | bytes 4325376 | tf_op jit(solution)/shard_map/grad_shards/pallas_call | solution.py:500
  211.1 1.6 collective-permute-start.52
  212.7 8.6 %grad_shards.3 = (bf16[4,288,768]{2,1,0:T(8,128)(2,1)}, bf16[4,288,768]{2,1,0:T(8,128)(2,1)}) custom-call(s32[11]{0:T(128)} %pad_add_fusion.info, bf16[1024,768]{1,0:T(8,128)(2,1)} %left.1, bf16[3,1024,768]{2,1,0:T(8,128)(2,1)} %get-tuple-element.51.grads.right), custom_call_target="tpu_custom_call" | custom-call | flops 3623878656 | bytes 9830400 | tf_op jit(solution)/shard_map/grad_shards/pallas_call | solution.py:500
  221.3 2.7 collective-permute-start.53
  224.0 8.8 %grad_tokens.1 = f32[1024,768]{1,0:T(8,128)} custom-call(f32[1024,768]{1,0:T(8,128)} %get-tuple-element.48.d_res, bf16[3,1024,768]{2,1,0:T(8,128)(2,1)} %get-tuple-element.51.grads.right, bf16[768,768]{1,0:T(8,128)(2,1)} %get-tuple-element.52.wq, bf16[768,768]{1,0:T(8,128)(2,1)} %get-tuple-element.53.wk, bf16[768,768]{1,0:T(8,128)(2,1)} %get-tuple-element.54.wv), custom_call_target="tpu_custom_call" | custom-call | flops 3623878656 | bytes 14548992 | tf_op jit(solution)/shard_map/grad_tokens/pallas_call | solution.py:531
  234.4 3.0 collective-permute-done.54
  237.9 4.4 %collective-permute-done.57 = bf16[192,768]{1,0:T(8,128)(2,1)S(1)} collective-permute-done((bf16[192,768]{1,0:T(8,128)(2,1)S(1)}, bf16[192,768]{1,0:T(8,128)(2,1)S(1)}, u32[]{:S(2)}, u32[]{:S(2)}) %collective-permute-start.57) | collective-permute-done | bytes 294944 | tf_op jit(solution)/shard_map/ppermute | solution.py:52
  242.3 1.6 collective-permute-start.58
  243.9 3.6 collective-permute-done.58
  248.2 3.9 %collective-permute-done.59 = bf16[48,768]{1,0:T(8,128)(2,1)S(1)} collective-permute-done((bf16[48,768]{1,0:T(8,128)(2,1)S(1)}, bf16[48,768]{1,0:T(8,128)(2,1)S(1)}, u32[]{:S(2)}, u32[]{:S(2)}) %collective-permute-start.59) | collective-permute-done | bytes 73760 | tf_op jit(solution)/shard_map/ppermute | solution.py:52
  252.1 2.7 collective-permute-start.60
  256.0 1.8 collective-permute-done.60
  257.7 2.0 collective-permute-start.61
  259.7 1.6 fusion.11
  261.4 1.6 collective-permute-start.43
  263.5 7.5 %grad_rows.3 = bf16[4,384,768]{2,1,0:T(8,128)(2,1)} custom-call(s32[11]{0:T(128)} %pad_add_fusion.info, bf16[1024,3072]{1,0:T(8,128)(2,1)} %get-tuple-element.67.left, bf16[1024,768]{1,0:T(8,128)(2,1)} %get-tuple-element.68.right, bf16[4,384,768]{2,1,0:T(8,128)(2,1)} %collective-permute-done.70.refs_0_), custom_call_target="tpu_custom_call" | custom-call | flops 2415919104 | bytes 7077888 | tf_op jit(solution)/shard_map/grad_rows/pallas_call | solution.py:454
  273.6 10.5 %collective-permute-done.43 = bf16[576,768]{1,0:T(8,128)(2,1)} collective-permute-done((bf16[576,768]{1,0:T(8,128)(2,1)S(1)}, bf16[576,768]{1,0:T(8,128)(2,1)}, u32[]{:S(2)}, u32[]{:S(2)}) %collective-permute-start.43) | collective-permute-done | bytes 884768 | tf_op jit(solution)/shard_map/ppermute | solution.py:52
  286.9 11.6 %collective-permute-done.44 = bf16[288,768]{1,0:T(8,128)(2,1)S(1)} collective-permute-done((bf16[288,768]{1,0:T(8,128)(2,1)S(1)}, bf16[288,768]{1,0:T(8,128)(2,1)S(1)}, u32[]{:S(2)}, u32[]{:S(2)}) %collective-permute-start.44) | collective-permute-done | bytes 442400 | tf_op jit(solution)/shard_map/ppermute | solution.py:52
  301.6 4.8 %collective-permute-done.45 = bf16[144,768]{1,0:T(8,128)(2,1)S(1)} collective-permute-done((bf16[144,768]{1,0:T(8,128)(2,1)S(1)}, bf16[144,768]{1,0:T(8,128)(2,1)S(1)}, u32[]{:S(2)}, u32[]{:S(2)}) %collective-permute-start.45) | collective-permute-done | bytes 221216 | tf_op jit(solution)/shard_map/ppermute | solution.py:52
  307.2 5.9 %collective-permute-done.46 = bf16[72,768]{1,0:T(8,128)(2,1)S(1)} collective-permute-done((bf16[72,768]{1,0:T(8,128)(2,1)S(1)}, bf16[72,768]{1,0:T(8,128)(2,1)S(1)}, u32[]{:S(2)}, u32[]{:S(2)}) %collective-permute-start.46) | collective-permute-done | bytes 110624 | tf_op jit(solution)/shard_map/ppermute | solution.py:52
  314.0 5.0 %collective-permute-done.47 = bf16[72,768]{1,0:T(8,128)(2,1)S(1)} collective-permute-done((bf16[72,768]{1,0:T(8,128)(2,1)S(1)}, bf16[72,768]{1,0:T(8,128)(2,1)S(1)}, u32[]{:S(2)}, u32[]{:S(2)}) %collective-permute-start.47) | collective-permute-done | bytes 110624 | tf_op jit(solution)/shard_map/ppermute | solution.py:52
  320.4 2.3 collective-permute-done.64
  322.9 1.6 collective-permute-start.65
  324.5 4.5 %collective-permute-done.48 = bf16[144,768]{1,0:T(8,128)(2,1)S(1)} collective-permute-done((bf16[144,768]{1,0:T(8,128)(2,1)S(1)}, bf16[144,768]{1,0:T(8,128)(2,1)S(1)}, u32[]{:S(2)}, u32[]{:S(2)}) %collective-permute-start.48) | collective-permute-done | bytes 221216 | tf_op jit(solution)/shard_map/ppermute | solution.py:52
  333.2 1.6 collective-permute-start.66
  334.9 5.4 %collective-permute-done.73 = bf16[192,768]{1,0:T(8,128)(2,1)S(1)} collective-permute-done((bf16[192,768]{1,0:T(8,128)(2,1)S(1)}, bf16[192,768]{1,0:T(8,128)(2,1)S(1)}, u32[]{:S(2)}, u32[]{:S(2)}) %collective-permute-start.73) | collective-permute-done | bytes 294944 | tf_op jit(solution)/shard_map/ppermute | solution.py:52
  340.7 8.2 %collective-permute-done.66 = bf16[48,3072]{1,0:T(8,128)(2,1)S(1)} collective-permute-done((bf16[48,3072]{1,0:T(8,128)(2,1)S(1)}, bf16[48,3072]{1,0:T(8,128)(2,1)S(1)}, u32[]{:S(2)}, u32[]{:S(2)}) %collective-permute-start.66) | collective-permute-done | bytes 294944 | tf_op jit(solution)/shard_map/ppermute | solution.py:52
  349.4 2.8 collective-permute-start.75
  352.2 5.4 %collective-permute-done.67 = bf16[24,3072]{1,0:T(8,128)(2,1)S(1)} collective-permute-done((bf16[24,3072]{1,0:T(8,128)(2,1)S(1)}, bf16[24,3072]{1,0:T(8,128)(2,1)S(1)}, u32[]{:S(2)}, u32[]{:S(2)}) %collective-permute-start.67) | collective-permute-done | bytes 147488 | tf_op jit(solution)/shard_map/ppermute | solution.py:52
  360.3 4.1 %collective-permute-done.68 = bf16[24,3072]{1,0:T(8,128)(2,1)S(1)} collective-permute-done((bf16[24,3072]{1,0:T(8,128)(2,1)S(1)}, bf16[24,3072]{1,0:T(8,128)(2,1)S(1)}, u32[]{:S(2)}, u32[]{:S(2)}) %collective-permute-start.68) | collective-permute-done | bytes 147488 | tf_op jit(solution)/shard_map/ppermute | solution.py:52
  364.5 2.9 collective-permute-done.76
  368.6 2.6 collective-permute-done.69
  (296 shorter events, 64.8 us)
Async XLA Ops:
  2.4 9.5 %collective-permute-start = (bf16[12,96]{1,0:T(8,128)(2,1)S(1)}, bf16[12,96]{1,0:T(8,128)(2,1)S(1)}, u32[]{:S(2)}, u32[]{:S(2)}) collective-permute-start(bf16[12,96]{1,0:T(8,128)(2,1)S(1)} %concatenate.62), channel_id=1, source_target_pairs={{0,1},{1,0},{2,3},{3,2},{4,5},{5,4},{6,7},{7,6},{8,9},{9,8},{10,11... | collective-permute-start | bytes 6920 | tf_op jit(solution)/shard_map/ppermute | solution.py:52
  2.9 9.0 %collective-permute-start.1 = (bf16[12,96]{1,0:T(8,128)(2,1)S(1)}, bf16[12,96]{1,0:T(8,128)(2,1)S(1)}, u32[]{:S(2)}, u32[]{:S(2)}) collective-permute-start(bf16[12,96]{1,0:T(8,128)(2,1)S(1)} %concatenate.62), channel_id=1, source_target_pairs={{0,2},{1,3},{2,0},{3,1},{4,6},{5,7},{6,4},{7,5},{8,10},{9,11},{10,... | collective-permute-start | bytes 6920 | tf_op jit(solution)/shard_map/ppermute | solution.py:52
  7.0 12.6 %collective-permute-start.22 = (bf16[96,768]{1,0:T(8,128)(2,1)}, bf16[96,768]{1,0:T(8,128)(2,1)S(1)}, u32[]{:S(2)}, u32[]{:S(2)}) collective-permute-start(bf16[96,768]{1,0:T(8,128)(2,1)} %refs_0_.1), channel_id=1, source_target_pairs={{0,2},{1,3},{2,0},{3,1},{4,6},{5,7},{6,4},{7,5},{8,10},{9,11},{10,... | collective-permute-start | bytes 442376 | tf_op jit(solution)/shard_map/ppermute | solution.py:52
  7.5 12.6 %collective-permute-start.24 = (bf16[96,768]{1,0:T(8,128)(2,1)}, bf16[96,768]{1,0:T(8,128)(2,1)S(1)}, u32[]{:S(2)}, u32[]{:S(2)}) collective-permute-start(bf16[96,768]{1,0:T(8,128)(2,1)} %refs_0_.1), channel_id=1, source_target_pairs={{0,4},{1,5},{2,6},{3,7},{4,0},{5,1},{6,2},{7,3},{8,12},{9,13},{10,... | collective-permute-start | bytes 442376 | tf_op jit(solution)/shard_map/ppermute | solution.py:52
  11.9 9.3 %collective-permute-start.21 = (bf16[96,768]{1,0:T(8,128)(2,1)}, bf16[96,768]{1,0:T(8,128)(2,1)S(1)}, u32[]{:S(2)}, u32[]{:S(2)}) collective-permute-start(bf16[96,768]{1,0:T(8,128)(2,1)} %refs_0_.1), channel_id=1, source_target_pairs={{0,1},{1,0},{2,3},{3,2},{4,5},{5,4},{6,7},{7,6},{8,9},{9,8},{10,11... | collective-permute-start | bytes 442376 | tf_op jit(solution)/shard_map/ppermute | solution.py:52
  18.1 13.8 %collective-permute-start.10 = (bf16[144,768]{1,0:T(8,128)(2,1)S(1)}, bf16[144,768]{1,0:T(8,128)(2,1)S(1)}, u32[]{:S(2)}, u32[]{:S(2)}) collective-permute-start(bf16[144,768]{1,0:T(8,128)(2,1)S(1)} %pad_maximum_fusion.6.refs_0_), channel_id=1, source_target_pairs={{0,4},{1,5},{2,6},{3,7},{4,0},{5,1},{6,2},{7,3},{8,12},{9,13},{10,... | collective-permute-start | bytes 663560 | tf_op jit(solution)/shard_map/ppermute | solution.py:52
  19.6 10.8 %collective-permute-start.17 = (bf16[144,768]{1,0:T(8,128)(2,1)S(1)}, bf16[144,768]{1,0:T(8,128)(2,1)S(1)}, u32[]{:S(2)}, u32[]{:S(2)}) collective-permute-start(bf16[144,768]{1,0:T(8,128)(2,1)S(1)} %pad_maximum_fusion.7.refs_8_), channel_id=1, source_target_pairs={{0,4},{1,5},{2,6},{3,7},{4,0},{5,1},{6,2},{7,3},{8,12},{9,13},{10,... | collective-permute-start | bytes 663560 | tf_op jit(solution)/shard_map/ppermute | solution.py:52
  20.1 11.8 %collective-permute-start.15 = (bf16[144,768]{1,0:T(8,128)(2,1)S(1)}, bf16[144,768]{1,0:T(8,128)(2,1)S(1)}, u32[]{:S(2)}, u32[]{:S(2)}) collective-permute-start(bf16[144,768]{1,0:T(8,128)(2,1)S(1)} %pad_maximum_fusion.7.refs_8_), channel_id=1, source_target_pairs={{0,2},{1,3},{2,0},{3,1},{4,6},{5,7},{6,4},{7,5},{8,10},{9,11},{10,... | collective-permute-start | bytes 663560 | tf_op jit(solution)/shard_map/ppermute | solution.py:52
  21.2 11.2 %collective-permute-start.14 = (bf16[144,768]{1,0:T(8,128)(2,1)S(1)}, bf16[144,768]{1,0:T(8,128)(2,1)S(1)}, u32[]{:S(2)}, u32[]{:S(2)}) collective-permute-start(bf16[144,768]{1,0:T(8,128)(2,1)S(1)} %pad_maximum_fusion.7.refs_8_), channel_id=1, source_target_pairs={{0,1},{1,0},{2,3},{3,2},{4,5},{5,4},{6,7},{7,6},{8,9},{9,8},{10,11... | collective-permute-start | bytes 663560 | tf_op jit(solution)/shard_map/ppermute | solution.py:52
  32.9 26.2 %collective-permute-start.29 = (bf16[96,3072]{1,0:T(8,128)(2,1)S(1)}, bf16[96,3072]{1,0:T(8,128)(2,1)S(1)}, u32[]{:S(2)}, u32[]{:S(2)}) collective-permute-start(bf16[96,3072]{1,0:T(8,128)(2,1)S(1)} %copy-done.8), channel_id=1, source_target_pairs={{0,2},{1,3},{2,0},{3,1},{4,6},{5,7},{6,4},{7,5},{8,10},{9,11},{10,... | collective-permute-start | bytes 1769480 | tf_op jit(solution)/shard_map/ppermute | solution.py:52
  36.0 16.8 %collective-permute-start.19 = (bf16[144,768]{1,0:T(8,128)(2,1)S(1)}, bf16[144,768]{1,0:T(8,128)(2,1)S(1)}, u32[]{:S(2)}, u32[]{:S(2)}) collective-permute-start(bf16[144,768]{1,0:T(8,128)(2,1)S(1)} %collective-permute-done.17.refs_12_), channel_id=1, source_target_pairs={{0,2},{1,3},{2,0},{3,1},{4,6},{5,7},{6,4},{7,5},{8,10},{9,11},{10,... | collective-permute-start | bytes 663560 | tf_op jit(solution)/shard_map/ppermute | solution.py:52
  37.0 17.3 %collective-permute-start.18 = (bf16[144,768]{1,0:T(8,128)(2,1)S(1)}, bf16[144,768]{1,0:T(8,128)(2,1)S(1)}, u32[]{:S(2)}, u32[]{:S(2)}) collective-permute-start(bf16[144,768]{1,0:T(8,128)(2,1)S(1)} %collective-permute-done.17.refs_12_), channel_id=1, source_target_pairs={{0,1},{1,0},{2,3},{3,2},{4,5},{5,4},{6,7},{7,6},{8,9},{9,8},{10,11... | collective-permute-start | bytes 663560 | tf_op jit(solution)/shard_map/ppermute | solution.py:52
  37.0 17.9 %collective-permute-start.9 = (bf16[144,768]{1,0:T(8,128)(2,1)S(1)}, bf16[144,768]{1,0:T(8,128)(2,1)S(1)}, u32[]{:S(2)}, u32[]{:S(2)}) collective-permute-start(bf16[144,768]{1,0:T(8,128)(2,1)S(1)} %collective-permute-done.8.refs_2_), channel_id=1, source_target_pairs={{0,1},{1,0},{2,3},{3,2},{4,5},{5,4},{6,7},{7,6},{8,9},{9,8},{10,11... | collective-permute-start | bytes 663560 | tf_op jit(solution)/shard_map/ppermute | solution.py:52
  40.3 15.8 %collective-permute-start.11 = (bf16[144,768]{1,0:T(8,128)(2,1)S(1)}, bf16[144,768]{1,0:T(8,128)(2,1)S(1)}, u32[]{:S(2)}, u32[]{:S(2)}) collective-permute-start(bf16[144,768]{1,0:T(8,128)(2,1)S(1)} %collective-permute-done.10.refs_4_), channel_id=1, source_target_pairs={{0,1},{1,0},{2,3},{3,2},{4,5},{5,4},{6,7},{7,6},{8,9},{9,8},{10,11... | collective-permute-start | bytes 663560 | tf_op jit(solution)/shard_map/ppermute | solution.py:52
  52.8 26.8 %collective-permute-start.31 = (bf16[96,3072]{1,0:T(8,128)(2,1)S(1)}, bf16[96,3072]{1,0:T(8,128)(2,1)S(1)}, u32[]{:S(2)}, u32[]{:S(2)}) collective-permute-start(bf16[96,3072]{1,0:T(8,128)(2,1)S(1)} %copy-done.8), channel_id=1, source_target_pairs={{0,4},{1,5},{2,6},{3,7},{4,0},{5,1},{6,2},{7,3},{8,12},{9,13},{10,... | collective-permute-start | bytes 1769480 | tf_op jit(solution)/shard_map/ppermute | solution.py:52
  54.3 25.3 %collective-permute-start.38 = (bf16[384,768]{1,0:T(8,128)(2,1)S(1)}, bf16[384,768]{1,0:T(8,128)(2,1)S(1)}, u32[]{:S(2)}, u32[]{:S(2)}) collective-permute-start(bf16[384,768]{1,0:T(8,128)(2,1)S(1)} %copy-done.9), channel_id=1, source_target_pairs={{0,4},{1,5},{2,6},{3,7},{4,0},{5,1},{6,2},{7,3},{8,12},{9,13},{10,... | collective-permute-start | bytes 1769480 | tf_op jit(solution)/shard_map/ppermute | solution.py:52
  54.9 25.2 %collective-permute-start.36 = (bf16[384,768]{1,0:T(8,128)(2,1)S(1)}, bf16[384,768]{1,0:T(8,128)(2,1)S(1)}, u32[]{:S(2)}, u32[]{:S(2)}) collective-permute-start(bf16[384,768]{1,0:T(8,128)(2,1)S(1)} %copy-done.9), channel_id=1, source_target_pairs={{0,2},{1,3},{2,0},{3,1},{4,6},{5,7},{6,4},{7,5},{8,10},{9,11},{10,... | collective-permute-start | bytes 1769480 | tf_op jit(solution)/shard_map/ppermute | solution.py:52
  59.0 22.7 %collective-permute-start.13 = (bf16[144,768]{1,0:T(8,128)(2,1)S(1)}, bf16[144,768]{1,0:T(8,128)(2,1)S(1)}, u32[]{:S(2)}, u32[]{:S(2)}) collective-permute-start(bf16[144,768]{1,0:T(8,128)(2,1)S(1)} %collective-permute-done.12.refs_6_), channel_id=1, source_target_pairs={{0,1},{1,0},{2,3},{3,2},{4,5},{5,4},{6,7},{7,6},{8,9},{9,8},{10,11... | collective-permute-start | bytes 663560 | tf_op jit(solution)/shard_map/ppermute | solution.py:52
  59.1 22.5 %collective-permute-start.20 = (bf16[144,768]{1,0:T(8,128)(2,1)S(1)}, bf16[144,768]{1,0:T(8,128)(2,1)S(1)}, u32[]{:S(2)}, u32[]{:S(2)}) collective-permute-start(bf16[144,768]{1,0:T(8,128)(2,1)S(1)} %collective-permute-done.19.refs_14_), channel_id=1, source_target_pairs={{0,1},{1,0},{2,3},{3,2},{4,5},{5,4},{6,7},{7,6},{8,9},{9,8},{10,11... | collective-permute-start | bytes 663560 | tf_op jit(solution)/shard_map/ppermute | solution.py:52
  79.6 15.5 %collective-permute-start.28 = (bf16[96,3072]{1,0:T(8,128)(2,1)S(1)}, bf16[96,3072]{1,0:T(8,128)(2,1)}, u32[]{:S(2)}, u32[]{:S(2)}) collective-permute-start(bf16[96,3072]{1,0:T(8,128)(2,1)S(1)} %copy-done.8), channel_id=1, source_target_pairs={{0,1},{1,0},{2,3},{3,2},{4,5},{5,4},{6,7},{7,6},{8,9},{9,8},{10,11... | collective-permute-start | bytes 1769480 | tf_op jit(solution)/shard_map/ppermute | solution.py:52
  79.6 15.7 %collective-permute-start.35 = (bf16[384,768]{1,0:T(8,128)(2,1)S(1)}, bf16[384,768]{1,0:T(8,128)(2,1)}, u32[]{:S(2)}, u32[]{:S(2)}) collective-permute-start(bf16[384,768]{1,0:T(8,128)(2,1)S(1)} %copy-done.9), channel_id=1, source_target_pairs={{0,1},{1,0},{2,3},{3,2},{4,5},{5,4},{6,7},{7,6},{8,9},{9,8},{10,11... | collective-permute-start | bytes 1769480 | tf_op jit(solution)/shard_map/ppermute | solution.py:52
  80.1 15.5 %collective-permute-start.33 = (bf16[96,3072]{1,0:T(8,128)(2,1)S(1)}, bf16[96,3072]{1,0:T(8,128)(2,1)}, u32[]{:S(2)}, u32[]{:S(2)}) collective-permute-start(bf16[96,3072]{1,0:T(8,128)(2,1)S(1)} %collective-permute-done.29.refs_10_), channel_id=1, source_target_pairs={{0,4},{1,5},{2,6},{3,7},{4,0},{5,1},{6,2},{7,3},{8,12},{9,13},{10,... | collective-permute-start | bytes 1769480 | tf_op jit(solution)/shard_map/ppermute | solution.py:52
  81.7 15.9 %collective-permute-start.30 = (bf16[96,3072]{1,0:T(8,128)(2,1)S(1)}, bf16[96,3072]{1,0:T(8,128)(2,1)}, u32[]{:S(2)}, u32[]{:S(2)}) collective-permute-start(bf16[96,3072]{1,0:T(8,128)(2,1)S(1)} %collective-permute-done.29.refs_10_), channel_id=1, source_target_pairs={{0,1},{1,0},{2,3},{3,2},{4,5},{5,4},{6,7},{7,6},{8,9},{9,8},{10,11... | collective-permute-start | bytes 1769480 | tf_op jit(solution)/shard_map/ppermute | solution.py:52
  81.7 15.9 %collective-permute-start.40 = (bf16[384,768]{1,0:T(8,128)(2,1)S(1)}, bf16[384,768]{1,0:T(8,128)(2,1)}, u32[]{:S(2)}, u32[]{:S(2)}) collective-permute-start(bf16[384,768]{1,0:T(8,128)(2,1)S(1)} %collective-permute-done.38.refs_20_), channel_id=1, source_target_pairs={{0,2},{1,3},{2,0},{3,1},{4,6},{5,7},{6,4},{7,5},{8,10},{9,11},{10,... | collective-permute-start | bytes 1769480 | tf_op jit(solution)/shard_map/ppermute | solution.py:52
  95.1 24.5 %collective-permute-start.39 = (bf16[384,768]{1,0:T(8,128)(2,1)S(1)}, bf16[384,768]{1,0:T(8,128)(2,1)S(1)}, u32[]{:S(2)}, u32[]{:S(2)}) collective-permute-start(bf16[384,768]{1,0:T(8,128)(2,1)S(1)} %collective-permute-done.38.refs_20_), channel_id=1, source_target_pairs={{0,1},{1,0},{2,3},{3,2},{4,5},{5,4},{6,7},{7,6},{8,9},{9,8},{10,11... | collective-permute-start | bytes 1769480 | tf_op jit(solution)/shard_map/ppermute | solution.py:52
  95.4 24.3 %collective-permute-start.32 = (bf16[96,3072]{1,0:T(8,128)(2,1)S(1)}, bf16[96,3072]{1,0:T(8,128)(2,1)S(1)}, u32[]{:S(2)}, u32[]{:S(2)}) collective-permute-start(bf16[96,3072]{1,0:T(8,128)(2,1)S(1)} %collective-permute-done.31.refs_12_), channel_id=1, source_target_pairs={{0,1},{1,0},{2,3},{3,2},{4,5},{5,4},{6,7},{7,6},{8,9},{9,8},{10,11... | collective-permute-start | bytes 1769480 | tf_op jit(solution)/shard_map/ppermute | solution.py:52
  95.7 24.0 %collective-permute-start.37 = (bf16[384,768]{1,0:T(8,128)(2,1)}, bf16[384,768]{1,0:T(8,128)(2,1)S(1)}, u32[]{:S(2)}, u32[]{:S(2)}) collective-permute-start(bf16[384,768]{1,0:T(8,128)(2,1)} %copy-done.13), channel_id=1, source_target_pairs={{0,1},{1,0},{2,3},{3,2},{4,5},{5,4},{6,7},{7,6},{8,9},{9,8},{10,11... | collective-permute-start | bytes 1769480 | tf_op jit(solution)/shard_map/ppermute | solution.py:52
  97.6 22.1 %collective-permute-start.34 = (bf16[96,3072]{1,0:T(8,128)(2,1)}, bf16[96,3072]{1,0:T(8,128)(2,1)}, u32[]{:S(2)}, u32[]{:S(2)}) collective-permute-start(bf16[96,3072]{1,0:T(8,128)(2,1)} %collective-permute-done.33.refs_14_), channel_id=1, source_target_pairs={{0,1},{1,0},{2,3},{3,2},{4,5},{5,4},{6,7},{7,6},{8,9},{9,8},{10,11... | collective-permute-start | bytes 1769480 | tf_op jit(solution)/shard_map/ppermute | solution.py:52
  97.6 22.1 %collective-permute-start.41 = (bf16[384,768]{1,0:T(8,128)(2,1)}, bf16[384,768]{1,0:T(8,128)(2,1)S(1)}, u32[]{:S(2)}, u32[]{:S(2)}) collective-permute-start(bf16[384,768]{1,0:T(8,128)(2,1)} %collective-permute-done.40.refs_22_), channel_id=1, source_target_pairs={{0,1},{1,0},{2,3},{3,2},{4,5},{5,4},{6,7},{7,6},{8,9},{9,8},{10,11... | collective-permute-start | bytes 1769480 | tf_op jit(solution)/shard_map/ppermute | solution.py:52
  193.5 70.0 %collective-permute-start.70 = (bf16[4,384,768]{2,1,0:T(8,128)(2,1)}, bf16[4,384,768]{2,1,0:T(8,128)(2,1)}, u32[]{:S(2)}, u32[]{:S(2)}) collective-permute-start(bf16[4,384,768]{2,1,0:T(8,128)(2,1)} %grad_rows.2), channel_id=1, source_target_pairs={{0,1},{1,0},{2,3},{3,2},{4,5},{5,4},{6,7},{7,6},{8,9},{9,8},{10,11... | collective-permute-start | bytes 7077896 | tf_op jit(solution)/shard_map/ppermute | solution.py:52
  194.0 11.2 %collective-permute-start.50 = (bf16[32,96]{1,0:T(8,128)(2,1)S(1)}, bf16[32,96]{1,0:T(8,128)(2,1)S(1)}, u32[]{:S(2)}, u32[]{:S(2)}) collective-permute-start(bf16[32,96]{1,0:T(8,128)(2,1)S(1)} %pad_maximum_fusion.10), channel_id=1, source_target_pairs={{0,2},{1,3},{2,0},{3,1},{4,6},{5,7},{6,4},{7,5},{8,10},{9,11},{10,... | collective-permute-start | bytes 18440 | tf_op jit(solution)/shard_map/ppermute | solution.py:52
  205.2 81.3 %collective-permute-start.63 = (bf16[4,96,3072]{2,1,0:T(8,128)(2,1)}, bf16[4,96,3072]{2,1,0:T(8,128)(2,1)S(1)}, u32[]{:S(2)}, u32[]{:S(2)}) collective-permute-start(bf16[4,96,3072]{2,1,0:T(8,128)(2,1)} %get-tuple-element.66), channel_id=1, source_target_pairs={{0,1},{1,0},{2,3},{3,2},{4,5},{5,4},{6,7},{7,6},{8,9},{9,8},{10,11... | collective-permute-start | bytes 7077896 | tf_op jit(solution)/shard_map/ppermute | solution.py:52
  210.8 22.4 %collective-permute-start.56 = (bf16[4,96,768]{2,1,0:T(8,128)(2,1)}, bf16[4,96,768]{2,1,0:T(8,128)(2,1)S(1)}, u32[]{:S(2)}, u32[]{:S(2)}) collective-permute-start(bf16[4,96,768]{2,1,0:T(8,128)(2,1)} %get-tuple-element.62), channel_id=1, source_target_pairs={{0,1},{1,0},{2,3},{3,2},{4,5},{5,4},{6,7},{7,6},{8,9},{9,8},{10,11... | collective-permute-start | bytes 1769480 | tf_op jit(solution)/shard_map/ppermute | solution.py:52
  211.1 10.2 %collective-permute-start.52 = (bf16[8,96]{1,0:T(8,128)(2,1)S(1)}, bf16[8,96]{1,0:T(8,128)(2,1)S(1)}, u32[]{:S(2)}, u32[]{:S(2)}) collective-permute-start(bf16[8,96]{1,0:T(8,128)(2,1)S(1)} %broadcast_select_fusion.26), channel_id=1, source_target_pairs={{0,8},{8,0},{16,24},{24,16},{1,9},{9,1},{17,25},{25,17},{2,10},{10... | collective-permute-start | bytes 4616 | tf_op jit(solution)/shard_map/ppermute | solution.py:52
  221.3 38.4 %collective-permute-start.42 = (bf16[4,288,768]{2,1,0:T(8,128)(2,1)}, bf16[4,288,768]{2,1,0:T(8,128)(2,1)}, u32[]{:S(2)}, u32[]{:S(2)}) collective-permute-start(bf16[4,288,768]{2,1,0:T(8,128)(2,1)} %get-tuple-element.56), channel_id=1, source_target_pairs={{0,1},{1,0},{2,3},{3,2},{4,5},{5,4},{6,7},{7,6},{8,9},{9,8},{10,11... | collective-permute-start | bytes 5308424 | tf_op jit(solution)/shard_map/ppermute | solution.py:52
  221.3 11.5 %collective-permute-start.53 = (bf16[4,96]{1,0:T(4,128)(2,1)S(1)}, bf16[4,96]{1,0:T(4,128)(2,1)S(1)}, u32[]{:S(2)}, u32[]{:S(2)}) collective-permute-start(bf16[4,96]{1,0:T(4,128)(2,1)S(1)} %broadcast_select_fusion.29), channel_id=1, source_target_pairs={{0,16},{8,24},{16,0},{24,8},{1,17},{9,25},{17,1},{25,9},{2,18},{10... | collective-permute-start | bytes 2312 | tf_op jit(solution)/shard_map/ppermute | solution.py:52
  261.4 22.7 %collective-permute-start.43 = (bf16[576,768]{1,0:T(8,128)(2,1)S(1)}, bf16[576,768]{1,0:T(8,128)(2,1)}, u32[]{:S(2)}, u32[]{:S(2)}) collective-permute-start(bf16[576,768]{1,0:T(8,128)(2,1)S(1)} %pad_maximum_fusion.2), channel_id=1, source_target_pairs={{0,4},{1,5},{2,6},{3,7},{4,0},{5,1},{6,2},{7,3},{8,12},{9,13},{10,... | collective-permute-start | bytes 2654216 | tf_op jit(solution)/shard_map/ppermute | solution.py:52
  263.0 44.2 %collective-permute-start.62 = (bf16[48,768]{1,0:T(8,128)(2,1)S(1)}, bf16[48,768]{1,0:T(8,128)(2,1)S(1)}, u32[]{:S(2)}, u32[]{:S(2)}) collective-permute-start(bf16[48,768]{1,0:T(8,128)(2,1)S(1)} %pad_maximum_fusion.9), channel_id=1, source_target_pairs={{0,8},{8,0},{16,24},{24,16},{1,9},{9,1},{17,25},{25,17},{2,10},{10... | collective-permute-start | bytes 221192 | tf_op jit(solution)/shard_map/ppermute | solution.py:52
  272.6 46.6 %collective-permute-start.71 = (bf16[768,768]{1,0:T(8,128)(2,1)S(1)}, bf16[768,768]{1,0:T(8,128)(2,1)S(1)}, u32[]{:S(2)}, u32[]{:S(2)}) collective-permute-start(bf16[768,768]{1,0:T(8,128)(2,1)S(1)} %pad_maximum_fusion.1), channel_id=1, source_target_pairs={{0,4},{1,5},{2,6},{3,7},{4,0},{5,1},{6,2},{7,3},{8,12},{9,13},{10,... | collective-permute-start | bytes 3538952 | tf_op jit(solution)/shard_map/ppermute | solution.py:52
  285.4 13.1 %collective-permute-start.44 = (bf16[288,768]{1,0:T(8,128)(2,1)S(1)}, bf16[288,768]{1,0:T(8,128)(2,1)S(1)}, u32[]{:S(2)}, u32[]{:S(2)}) collective-permute-start(bf16[288,768]{1,0:T(8,128)(2,1)S(1)} %fusion.4), channel_id=1, source_target_pairs={{0,2},{1,3},{2,0},{3,1},{4,6},{5,7},{6,4},{7,5},{8,10},{9,11},{10,... | collective-permute-start | bytes 1327112 | tf_op jit(solution)/shard_map/ppermute | solution.py:52
  300.6 22.1 %collective-permute-start.64 = (bf16[192,3072]{1,0:T(8,128)(2,1)S(1)}, bf16[192,3072]{1,0:T(8,128)(2,1)S(1)}, u32[]{:S(2)}, u32[]{:S(2)}) collective-permute-start(bf16[192,3072]{1,0:T(8,128)(2,1)S(1)} %pad_maximum_fusion), channel_id=1, source_target_pairs={{0,2},{1,3},{2,0},{3,1},{4,6},{5,7},{6,4},{7,5},{8,10},{9,11},{10,... | collective-permute-start | bytes 3538952 | tf_op jit(solution)/shard_map/ppermute | solution.py:52
  319.1 9.9 %collective-permute-start.48 = (bf16[144,768]{1,0:T(8,128)(2,1)S(1)}, bf16[144,768]{1,0:T(8,128)(2,1)S(1)}, u32[]{:S(2)}, u32[]{:S(2)}) collective-permute-start(bf16[144,768]{1,0:T(8,128)(2,1)S(1)} %pad_maximum_fusion.8), channel_id=1, source_target_pairs={{0,8},{8,0},{16,24},{24,16},{1,9},{9,1},{17,25},{25,17},{2,10},{10... | collective-permute-start | bytes 663560 | tf_op jit(solution)/shard_map/ppermute | solution.py:52
  319.3 10.8 %collective-permute-start.72 = (bf16[384,768]{1,0:T(8,128)(2,1)S(1)}, bf16[384,768]{1,0:T(8,128)(2,1)S(1)}, u32[]{:S(2)}, u32[]{:S(2)}) collective-permute-start(bf16[384,768]{1,0:T(8,128)(2,1)S(1)} %fusion), channel_id=1, source_target_pairs={{0,2},{1,3},{2,0},{3,1},{4,6},{5,7},{6,4},{7,5},{8,10},{9,11},{10,... | collective-permute-start | bytes 1769480 | tf_op jit(solution)/shard_map/ppermute | solution.py:52
  322.9 9.9 %collective-permute-start.65 = (bf16[96,3072]{1,0:T(8,128)(2,1)S(1)}, bf16[96,3072]{1,0:T(8,128)(2,1)S(1)}, u32[]{:S(2)}, u32[]{:S(2)}) collective-permute-start(bf16[96,3072]{1,0:T(8,128)(2,1)S(1)} %fusion.2), channel_id=1, source_target_pairs={{0,4},{1,5},{2,6},{3,7},{4,0},{5,1},{6,2},{7,3},{8,12},{9,13},{10,... | collective-permute-start | bytes 1769480 | tf_op jit(solution)/shard_map/ppermute | solution.py:52
  330.4 9.9 %collective-permute-start.73 = (bf16[192,768]{1,0:T(8,128)(2,1)S(1)}, bf16[192,768]{1,0:T(8,128)(2,1)S(1)}, u32[]{:S(2)}, u32[]{:S(2)}) collective-permute-start(bf16[192,768]{1,0:T(8,128)(2,1)S(1)} %broadcast_select_fusion.2), channel_id=1, source_target_pairs={{0,8},{8,0},{16,24},{24,16},{1,9},{9,1},{17,25},{25,17},{2,10},{10... | collective-permute-start | bytes 884744 | tf_op jit(solution)/shard_map/ppermute | solution.py:52
  333.2 15.7 %collective-permute-start.66 = (bf16[48,3072]{1,0:T(8,128)(2,1)S(1)}, bf16[48,3072]{1,0:T(8,128)(2,1)S(1)}, u32[]{:S(2)}, u32[]{:S(2)}) collective-permute-start(bf16[48,3072]{1,0:T(8,128)(2,1)S(1)} %broadcast_select_fusion.5), channel_id=1, source_target_pairs={{0,8},{8,0},{16,24},{24,16},{1,9},{9,1},{17,25},{25,17},{2,10},{10... | collective-permute-start | bytes 884744 | tf_op jit(solution)/shard_map/ppermute | solution.py:52
  340.4 9.0 %collective-permute-start.74 = (bf16[96,768]{1,0:T(8,128)(2,1)S(1)}, bf16[96,768]{1,0:T(8,128)(2,1)S(1)}, u32[]{:S(2)}, u32[]{:S(2)}) collective-permute-start(bf16[96,768]{1,0:T(8,128)(2,1)S(1)} %broadcast_select_fusion.11), channel_id=1, source_target_pairs={{0,16},{8,24},{16,0},{24,8},{1,17},{9,25},{17,1},{25,9},{2,18},{10... | collective-permute-start | bytes 442376 | tf_op jit(solution)/shard_map/ppermute | solution.py:52
  349.4 9.7 %collective-permute-start.75 = (bf16[96,768]{1,0:T(8,128)(2,1)S(1)}, bf16[96,768]{1,0:T(8,128)(2,1)S(1)}, u32[]{:S(2)}, u32[]{:S(2)}) collective-permute-start(bf16[96,768]{1,0:T(8,128)(2,1)S(1)} %add_convert_fusion.14), channel_id=1, source_target_pairs={{0,16},{8,24},{16,0},{24,8},{1,17},{9,25},{17,1},{25,9},{2,18},{10... | collective-permute-start | bytes 442376 | tf_op jit(solution)/shard_map/ppermute | solution.py:52
  (65 other events, 1089.1 us)
